TPU v7x, 32 devices: a whole 2x2x4 slice. The times are simulated.
32 devices in a mesh: dp: 8 (over z, x), tp: 4 (over y, core).
Axes of the slice: x: 2, y: 2, z: 4, core: 2. Of those that a mesh axis runs over, the one named last changes fastest.
Arguments:
- layer_input: bfloat16 [4096, 768], P('dp'), may hold values from -6 to 6
- pair_lengths: int32 [16], P('dp'), may hold values from 32 to 256, as said below
- query_weight: bfloat16 [768, 768], P('dp', 'tp'), may hold values from -0.21875 to 0.21875
- query_bias: float32 [768], P('tp'), may hold values from -3 to 3
- key_weight: bfloat16 [768, 768], P('dp', 'tp'), may hold values from -0.21875 to 0.21875
- value_weight: bfloat16 [768, 768], P('dp', 'tp'), may hold values from -0.21875 to 0.21875
- value_bias: float32 [768], P('tp'), may hold values from -3 to 3
- out_weight: bfloat16 [768, 768], P('tp', 'dp'), may hold values from -1.5 to 1.5
- out_bias: float32 [768], replicated, may hold values from -3 to 3
- first_gain: float32 [768], replicated, may hold values from 0.5 to 1.5
- first_shift: float32 [768], replicated, may hold values from -2 to 2
- up_weight: bfloat16 [768, 3072], P('dp', 'tp'), may hold values from -0.21875 to 0.21875
- up_bias: float32 [3072], P('tp'), may hold values from -3 to 3
- down_weight: bfloat16 [3072, 768], P('tp', 'dp'), may hold values from -0.21875 to 0.21875
- down_bias: float32 [768], replicated, may hold values from -3 to 3
- second_gain: float32 [768], replicated, may hold values from 0.5 to 1.5
- second_shift: float32 [768], replicated, may hold values from -2 to 2
- out_grad: bfloat16 [4096, 768], P('dp'), may hold values from -6 to 6
- query_tangent: bfloat16 [768, 768], P('dp', 'tp'), may hold values from -0.21875 to 0.21875
- key_tangent: bfloat16 [768, 768], P('dp', 'tp'), may hold values from -0.21875 to 0.21875
- value_tangent: bfloat16 [768, 768], P('dp', 'tp'), may hold values from -0.21875 to 0.21875
- out_tangent: bfloat16 [768, 768], P('tp', 'dp'), may hold values from -1.5 to 1.5
- up_tangent: bfloat16 [768, 3072], P('dp', 'tp'), may hold values from -0.21875 to 0.21875
- down_tangent: bfloat16 [3072, 768], P('tp', 'dp'), may hold values from -0.21875 to 0.21875
Outputs:
- layer_output: bfloat16 [4096, 768], P('dp')
- input_grad: bfloat16 [4096, 768], P('dp')
- layer_output_jvp: bfloat16 [4096, 768], P('dp')
- query_weight_grad: float32 [768, 768], P('dp', 'tp')
- query_bias_grad: float32 [768], P('tp')
- key_weight_grad: float32 [768, 768], P('dp', 'tp')
- value_weight_grad: float32 [768, 768], P('dp', 'tp')
- value_bias_grad: float32 [768], P('tp')
- out_weight_grad: float32 [768, 768], P('tp', 'dp')
- out_bias_grad: float32 [768], replicated
- first_gain_grad: float32 [768], replicated
- first_shift_grad: float32 [768], replicated
- up_weight_grad: float32 [768, 3072], P('dp', 'tp')
- up_bias_grad: float32 [3072], P('tp')
- down_weight_grad: float32 [3072, 768], P('tp', 'dp')
- down_bias_grad: float32 [768], replicated
- second_gain_grad: float32 [768], replicated
- second_shift_grad: float32 [768], replicated
Inputs may be any that keep to these rules, and one draw needn't show every extreme that they name: Slots 0 to pair_lengths[p] - 1 of pair p hold tokens, the rest are padding; some pair has length 256.
All inputs are finite; a program needn't handle non-finite values.
Results may differ from a plain program's by a relative error of at most 0.024.
Values may be sent and summed in bfloat16 or wider, within the bound.
No kernel may reach another device: no remote copies, remote signals or barrier semaphores. Data moves between devices by JAX's collectives and lax.ppermute only.
A program may use at most 128 MiB of HBM per device.

v0:
```python
import jax
import jax.numpy as jnp
from jax import lax
from jax.sharding import PartitionSpec as P

HEAD = 64
SEQ = 256
EPSILON = 1e-06
SNAKE = (0, 2, 4, 6, 7, 5, 3, 1)
BF = jnp.bfloat16
F32 = jnp.float32


def dot(left, right, dims):
    return lax.dot_general(left, right, (dims, ((), ())), preferred_element_type=F32)


NN = ((1,), (0,))
NT = ((1,), (1,))
TN = ((0,), (0,))


def xor_pairs(size, bit):
    return [(i, i ^ bit) for i in range(size)]


def gather_rows(shard, dp):
    if dp != len(SNAKE):
        return lax.all_gather(shard, "dp", axis=0, tiled=True)
    size = len(SNAKE)
    ahead = [(SNAKE[i], SNAKE[(i + 1) % size]) for i in range(size)]
    behind = [(b, a) for a, b in ahead]
    place = [0] * size
    for position, device in enumerate(SNAKE):
        place[device] = position
    me = lax.axis_index("dp")
    own_place = jnp.array(place, jnp.int32)[me]
    order = jnp.array(SNAKE, jnp.int32)
    rows = shard.shape[0]
    whole = jnp.zeros((size * rows, shard.shape[1]), shard.dtype)
    whole = lax.dynamic_update_slice(whole, shard, (me * rows, 0))
    one = two = shard
    for step in range(1, size // 2 + 1):
        one = lax.ppermute(one, "dp", ahead)
        owner = order[(own_place - step) % size]
        whole = lax.dynamic_update_slice(whole, one, (owner * rows, 0))
        if step < size // 2:
            two = lax.ppermute(two, "dp", behind)
            owner = order[(own_place + step) % size]
            whole = lax.dynamic_update_slice(whole, two, (owner * rows, 0))
    return whole


def scatter_sum(part, tp):
    count, rows, width = part.shape
    me = lax.axis_index("tp")
    rest = part.reshape(count, tp, rows // tp, width)
    size = tp
    bit = 1
    while bit < tp:
        size = size // 2
        split = rest.reshape(count, size, 2, rows // tp, width)
        mine = me // bit % 2
        keep = lax.dynamic_index_in_dim(split, mine, 2, keepdims=False)
        send = lax.dynamic_index_in_dim(split, 1 - mine, 2, keepdims=False)
        came = lax.ppermute(send.astype(BF), "tp", xor_pairs(tp, bit))
        rest = keep.astype(F32) + came.astype(F32)
        bit = bit * 2
        if bit < tp:
            rest = rest.astype(BF)
    return rest.reshape(count, rows // tp, width)


def norm_parts(resid):
    center = resid - jnp.mean(resid, axis=-1, keepdims=True)
    inverse = lax.rsqrt(jnp.mean(center * center, axis=-1, keepdims=True) + EPSILON)
    return (center * inverse, inverse)


def norm_along(unit, inverse, along):
    shifted = along - jnp.mean(along, axis=-1, keepdims=True)
    return inverse * (shifted - unit * jnp.mean(unit * shifted, axis=-1, keepdims=True))


def per_device(tp, dp, *arrays):
    (
        layer_input,
        pair_lengths,
        query_weight,
        query_bias,
        key_weight,
        value_weight,
        value_bias,
        out_weight,
        out_bias,
        first_gain,
        first_shift,
        up_weight,
        up_bias,
        down_weight,
        down_bias,
        second_gain,
        second_shift,
        out_grad,
        query_tangent,
        key_tangent,
        value_tangent,
        out_tangent,
        up_tangent,
        down_tangent,
    ) = arrays
    rows, width = layer_input.shape
    pairs = rows // SEQ
    cols = query_weight.shape[1]
    hidden = up_weight.shape[1]
    heads = cols // HEAD
    scale = HEAD ** (-0.5)
    me = lax.axis_index("tp")
    own_rows = rows // tp
    attn = gather_rows(
        jnp.concatenate(
            [query_weight, key_weight, value_weight, query_tangent, key_tangent, value_tangent], 1
        ),
        dp,
    )
    outs = gather_rows(jnp.concatenate([out_weight.T, out_tangent.T], 1), dp)
    ups = gather_rows(jnp.concatenate([up_weight, up_tangent], 1), dp)
    downs = gather_rows(jnp.concatenate([down_weight.T, down_tangent.T], 1), dp)
    out_full, tout_full = (outs[:, :cols], outs[:, cols:])
    up_full, tup_full = (ups[:, :hidden], ups[:, hidden:])
    down_full, tdown_full = (downs[:, :hidden], downs[:, hidden:])
    rows_own = lax.dynamic_slice_in_dim(layer_input, me * own_rows, own_rows, 0).astype(F32)
    upstream = lax.dynamic_slice_in_dim(out_grad, me * own_rows, own_rows, 0).astype(F32)
    zeros = jnp.zeros((cols,), F32)
    shift_all = jnp.concatenate([query_bias, zeros, value_bias, zeros, zeros, zeros])
    mixed = (dot(layer_input, attn, NN) + shift_all).astype(BF)
    mixed = mixed.reshape(pairs, SEQ, 6, heads, HEAD)
    query, key, value, tquery, tkey, tvalue = [mixed[:, :, i] for i in range(6)]
    valid = (
        lax.broadcasted_iota(jnp.int32, (pairs, 1, 1, SEQ), 3) < pair_lengths[:, None, None, None]
    )

    def ein(text, left, right):
        return jnp.einsum(text, left, right, preferred_element_type=F32)

    scores = jnp.where(valid, ein("pqhd,pkhd->phqk", query, key) * scale, jnp.float32(-1e30))
    expo = jnp.exp(scores - jnp.max(scores, axis=-1, keepdims=True))
    probs = expo / jnp.sum(expo, axis=-1, keepdims=True)
    probs_low = probs.astype(BF)
    context = ein("phqk,pkhd->pqhd", probs_low, value).reshape(rows, cols).astype(BF)
    tscores = ein("pqhd,pkhd->phqk", tquery, key) + ein("pqhd,pkhd->phqk", query, tkey)
    tscores = jnp.where(valid, tscores * scale, jnp.float32(0.0))
    tprobs = probs * (tscores - jnp.sum(tscores * probs, axis=-1, keepdims=True))
    tcontext = ein("phqk,pkhd->pqhd", tprobs.astype(BF), value)
    tcontext = tcontext + ein("phqk,pkhd->pqhd", probs_low, tvalue)
    tcontext = tcontext.reshape(rows, cols).astype(BF)
    part = dot(context, out_full, NT).astype(BF)
    tpart = (dot(tcontext, out_full, NT) + dot(context, tout_full, NT)).astype(BF)
    attended, tattended = scatter_sum(jnp.stack([part, tpart]), tp)
    unit_one, inverse_one = norm_parts(rows_own + attended + out_bias)
    first = unit_one * first_gain + first_shift
    tfirst = norm_along(unit_one, inverse_one, tattended) * first_gain
    first_low = lax.all_gather(first.astype(BF), "tp", axis=0, tiled=True)
    tfirst_low = lax.all_gather(tfirst.astype(BF), "tp", axis=0, tiled=True)
    upper = dot(first_low, up_full, NN) + up_bias
    tupper = dot(tfirst_low, up_full, NN) + dot(first_low, tup_full, NN)
    half = 0.5 * (1.0 + lax.erf(upper * 2.0 ** (-0.5)))
    active = (upper * half).astype(BF)
    slope = half + upper * (jnp.exp(-0.5 * upper * upper) * (2.0 * jnp.pi) ** (-0.5))
    tactive = (slope * tupper).astype(BF)
    part = dot(active, down_full, NT).astype(BF)
    tpart = (dot(tactive, down_full, NT) + dot(active, tdown_full, NT)).astype(BF)
    lowered, tlowered = scatter_sum(jnp.stack([part, tpart]), tp)
    unit_two, inverse_two = norm_parts(first + lowered + down_bias)
    result = (unit_two * second_gain + second_shift).astype(BF)
    tresult = (norm_along(unit_two, inverse_two, tfirst + tlowered) * second_gain).astype(BF)
    gain_two = jnp.sum(upstream * unit_two, axis=0)
    shift_two = jnp.sum(upstream, axis=0)
    grad_two = norm_along(unit_two, inverse_two, upstream * second_gain)
    bias_two = jnp.sum(grad_two, axis=0)
    grad_down = lax.all_gather(grad_two.astype(BF), "tp", axis=0, tiled=True)
    grad_active = dot(grad_down, down_full, NN)
    grad_upper = grad_active * slope
    bias_up = jnp.sum(grad_upper, axis=0)
    grad_upper_low = grad_upper.astype(BF)
    step_down = dot(grad_down, active, TN).astype(BF)
    step_up = dot(first_low, grad_upper_low, TN).astype(BF)
    part = dot(grad_upper_low, up_full, NT).astype(BF)
    (grad_first,) = scatter_sum(part[None], tp)
    grad_first = grad_first + grad_two
    gain_one = jnp.sum(grad_first * unit_one, axis=0)
    shift_one = jnp.sum(grad_first, axis=0)
    grad_one = norm_along(unit_one, inverse_one, grad_first * first_gain)
    bias_out = jnp.sum(grad_one, axis=0)
    grad_attn = lax.all_gather(grad_one.astype(BF), "tp", axis=0, tiled=True)
    step_out = dot(grad_attn, context, TN).astype(BF)
    grad_context = dot(grad_attn, out_full, NN).astype(BF).reshape(pairs, SEQ, heads, HEAD)
    grad_values = ein("phqk,pqhd->pkhd", probs_low, grad_context).astype(BF)
    grad_probs = ein("pqhd,pkhd->phqk", grad_context, value)
    grad_scores = probs * (grad_probs - jnp.sum(grad_probs * probs, axis=-1, keepdims=True))
    grad_scores = grad_scores.astype(BF)
    grad_queries = (ein("phqk,pkhd->pqhd", grad_scores, key) * scale).astype(BF)
    grad_keys = (ein("phqk,pqhd->pkhd", grad_scores, query) * scale).astype(BF)
    grad_mixed = jnp.concatenate(
        [g.reshape(rows, cols) for g in (grad_queries, grad_keys, grad_values)], 1
    )
    step_mixed = dot(layer_input, grad_mixed, TN).astype(BF)
    bias_mixed = jnp.sum(grad_mixed.astype(F32), axis=0)
    part = dot(grad_mixed, attn[:, : 3 * cols], NT).astype(BF)
    (grad_input,) = scatter_sum(part[None], tp)
    grad_input = (grad_input + grad_one).astype(BF)

    def spread(step):
        split = step.reshape(dp, step.shape[0] // dp, step.shape[1])
        came = lax.all_to_all(split, "dp", 0, 0, tiled=True)
        return jnp.sum(came.astype(F32), axis=0)

    own_down = spread(step_down).T
    own_up = spread(step_up)
    own_out = spread(step_out).T
    own_mixed = spread(step_mixed)
    small = jnp.concatenate(
        [bias_out, gain_one, shift_one, bias_two, gain_two, shift_two, bias_up, bias_mixed]
    )
    pad = -small.shape[0] % 128
    small = jnp.concatenate([small, jnp.zeros((pad,), F32)]).reshape(1, -1, 128)
    small = lax.all_to_all(jnp.broadcast_to(small, (dp,) + small.shape[1:]), "dp", 0, 0, tiled=True)
    small = jnp.sum(small, axis=0)
    shared = 6 * width // 128
    common = lax.all_gather(small[:shared], "tp", axis=0, tiled=False)
    common = jnp.sum(common, axis=0).reshape(6, width)
    small = small[shared:].reshape(-1)

    def all_rows(block):
        return lax.all_gather(block, "tp", axis=0, tiled=True)

    return (
        all_rows(result),
        all_rows(grad_input),
        all_rows(tresult),
        own_mixed[:, :cols],
        small[hidden : hidden + cols],
        own_mixed[:, cols : 2 * cols],
        own_mixed[:, 2 * cols :],
        small[hidden + 2 * cols : hidden + 3 * cols],
        own_out,
        common[0],
        common[1],
        common[2],
        own_up,
        small[:hidden],
        own_down,
        common[3],
        common[4],
        common[5],
    )


def solution(mesh):
    wide, tall, col, row, full = (P("dp", "tp"), P("tp", "dp"), P("tp"), P("dp", None), P())
    placed = (row, P("dp"), wide, col, wide, wide, col, tall, full, full, full, wide, col, tall) + (
        full,
        full,
        full,
        row,
        wide,
        wide,
        wide,
        tall,
        wide,
        tall,
    )
    results = (row, row, row, wide, col, wide, wide, col, tall, full, full, full)
    results = results + (wide, col, tall, full, full, full)
    tp, dp = (mesh.shape["tp"], mesh.shape["dp"])

    def body(*arrays):
        return per_device(tp, dp, *arrays)

    return jax.shard_map(body, mesh=mesh, in_specs=placed, out_specs=results, check_vma=False)
```

profile of v0, /device:TPU:0, one launch (start us, length us, event | category | flops | bytes accessed | tf_op | source)
XLA Modules:
  0.0 347.0 jit_solution(11669292654470791537)
XLA Ops:
  3.2 3.0 collective-permute-start.23
  6.2 2.1 collective-permute-start.7
  8.5 2.1 collective-permute-start
  13.1 3.0 collective-permute-done.7
  16.1 2.1 collective-permute-start.9
  32.6 1.7 collective-permute-start.16
  37.4 2.1 collective-permute-start.11
  39.5 3.1 collective-permute-done.1
  43.6 2.3 collective-permute-start.17
  47.6 2.0 collective-permute-start.2
  53.0 2.0 collective-permute-start.13
  56.7 2.0 collective-permute-done.13
  58.7 1.8 collective-permute-start.25
  63.2 1.7 collective-permute-start.18
  67.0 1.8 collective-permute-start.4
  71.8 3.5 %collective-permute-done.18 = bf16[96,1536]{1,0:T(8,128)(2,1)} collective-permute-done((bf16[96,1536]{1,0:T(8,128)(2,1)}, bf16[96,1536]{1,0:T(8,128)(2,1)}, u32[]{:S(2)}, u32[]{:S(2)}) %collective-permute-start.18) | collective-permute-done | bytes 294944 | tf_op jit(solution)/shard_map/ppermute | solution.py:44
  78.4 2.2 collective-permute-start.20
  82.8 1.9 collective-permute-start.6
  84.7 6.0 %collective-permute-done.6 = bf16[96,1152]{1,0:T(8,128)(2,1)S(1)} collective-permute-done((bf16[96,1152]{1,0:T(8,128)(2,1)S(1)}, bf16[96,1152]{1,0:T(8,128)(2,1)S(1)}, u32[]{:S(2)}, u32[]{:S(2)}) %collective-permute-start.6) | collective-permute-done | bytes 221216 | tf_op jit(solution)/shard_map/ppermute | solution.py:44
  90.7 2.2 fusion.2
  92.9 2.9 reshape.362
  95.8 1.8 fusion.87
  97.6 1.8 fusion.91
  106.1 1.7 constant_dynamic-update-slice_fusion.5
  109.3 1.7 constant_dynamic-update-slice_fusion.14
  111.0 1.9 collective-permute-start.22
  112.9 1.8 constant_dynamic-update-slice_fusion.10
  114.7 1.9 constant_dynamic-update-slice_fusion.12
  118.4 5.3 %collective-permute-done.22 = bf16[96,1536]{1,0:T(8,128)(2,1)S(1)} collective-permute-done((bf16[96,1536]{1,0:T(8,128)(2,1)}, bf16[96,1536]{1,0:T(8,128)(2,1)S(1)}, u32[]{:S(2)}, u32[]{:S(2)}) %collective-permute-start.22) | collective-permute-done | bytes 294944 | tf_op jit(solution)/shard_map/ppermute | solution.py:44
  125.3 2.6 collective-permute-done.15
  128.9 8.6 %all_gather.27 = bf16[512,768]{1,0:T(8,128)(2,1)S(1)} all-gather(bf16[128,768]{1,0:T(8,128)(2,1)S(1)} %get-tuple-element.46), channel_id=1, replica_groups=mesh['dp'=8,'tp'=4] {'tp'}, dimensions={0}, use_global_device_ids=true | all-gather | bytes 983040 | tf_op jit(solution)/shard_map/all_gather | solution.py:163
  137.5 3.5 %fusion.14 = f32[512,768]{1,0:T(8,128)} fusion(bf16[512,768]{1,0:T(8,128)(2,1)S(1)} %all_gather.27, bf16[768,1536]{1,0:T(8,128)(2,1)} %constant_dynamic-update-slice_fusion.13), kind=kOutput, calls=%fused_computation.53 | convolution fusion | flops 603979776 | bytes 3538944 | tf_op jit(solution)/shard_map/dot_general | solution.py:15
  141.0 3.3 multiply_convert_fusion.2
  144.3 3.6 %fusion.12 = f32[512,768]{1,0:T(8,128)} fusion(bf16[512,768]{1,0:T(8,128)(2,1)S(1)} %get-tuple-element.71, bf16[768,1536]{1,0:T(8,128)(2,1)} %constant_dynamic-update-slice_fusion.20), kind=kOutput, calls=%fused_computation.51 | convolution fusion | flops 603979776 | bytes 3538944 | tf_op jit(solution)/shard_map/dot_general | solution.py:15
  147.9 2.1 convolution_convert_fusion.4
  150.0 9.4 %all_gather.28 = bf16[512,768]{1,0:T(8,128)(2,1)} all-gather(bf16[128,768]{1,0:T(8,128)(2,1)S(1)} %get-tuple-element.33), channel_id=1, replica_groups=mesh['dp'=8,'tp'=4] {'tp'}, dimensions={0}, use_global_device_ids=true | all-gather | bytes 983040 | tf_op jit(solution)/shard_map/all_gather | solution.py:164
  159.4 4.9 %add_convert_fusion = bf16[512,768]{1,0:T(8,128)(2,1)S(1)} fusion(f32[512,768]{1,0:T(8,128)} %fusion.12, bf16[768,1536]{1,0:T(8,128)(2,1)} %constant_dynamic-update-slice_fusion.20, f32[512,768]{1,0:T(8,128)} %fusion.14, bf16[512,768]{1,0:T(8,128)(2,1)} %all_gather.28, bf16[768,1536]{1,0:T(8,128)(2,1)} %constant_dynamic-update-slice_fusion.13, ...), kind=kOutput, calls=%fused_computation.27 | convolution fusion | flops 1213071360 | bytes 8650752 | tf_op jit(solution)/shard_map/dot_general | solution.py:15
  164.8 1.9 collective-permute-done.30
  167.7 10.7 %collective-permute-done.31 = bf16[2,1,128,768]{3,2,1,0:T(8,128)(2,1)S(1)} collective-permute-done((bf16[2,1,128,768]{3,2,1,0:T(8,128)(2,1)S(1)}, bf16[2,1,128,768]{3,2,1,0:T(8,128)(2,1)S(1)}, u32[]{:S(2)}, u32[]{:S(2)}) %collective-permute-start.31) | collective-permute-done | bytes 393248 | tf_op jit(solution)/shard_map/ppermute | solution.py:66
  179.7 8.0 %all_gather.30 = bf16[512,768]{1,0:T(8,128)(2,1)S(1)} all-gather(bf16[128,768]{1,0:T(8,128)(2,1)S(1)} %convert_element_type.267), channel_id=1, replica_groups=mesh['dp'=8,'tp'=4] {'tp'}, dimensions={0}, use_global_device_ids=true | all-gather | bytes 983040 | tf_op jit(solution)/shard_map/all_gather | solution.py:181
  187.7 2.6 fusion.92
  190.4 2.4 convolution_convert_fusion.3
  196.0 5.9 %collective-permute-done.33 = bf16[1,1,128,768]{3,2,1,0:T(8,128)(2,1)S(1)} collective-permute-done((bf16[1,1,128,768]{3,2,1,0:T(8,128)(2,1)S(1)}, bf16[1,1,128,768]{3,2,1,0:T(8,128)(2,1)S(1)}, u32[]{:S(2)}, u32[]{:S(2)}) %collective-permute-start.33) | collective-permute-done | bytes 196640 | tf_op jit(solution)/shard_map/ppermute | solution.py:66
  202.5 8.3 %all_gather.31 = bf16[512,768]{1,0:T(8,128)(2,1)S(1)} all-gather(bf16[128,768]{1,0:T(8,128)(2,1)S(1)} %convert_element_type.276), channel_id=1, replica_groups=mesh['dp'=8,'tp'=4] {'tp'}, dimensions={0}, use_global_device_ids=true | all-gather | bytes 983040 | tf_op jit(solution)/shard_map/all_gather | solution.py:195
  211.4 1.9 fusion.20
  217.0 3.4 all-to-all-start.1
  222.1 7.1 %all-to-all-done.1 = f32[8,47,128]{2,1,0:T(8,128)S(1)} async-done(((f32[8,47,128]{2,1,0:T(8,128)}), f32[8,47,128]{2,1,0:T(8,128)S(1)}, u32[]{:S(2)}, u32[]{:S(2)}) %all-to-all-start.1) | async-done | bytes 192544 | tf_op jit(solution)/shard_map/all_to_all | solution.py:227
  229.1 3.5 all-to-all-start.2
  232.6 3.0 convolution_convert_fusion
  235.6 8.6 %all-to-all-done.2 = bf16[8,96,192]{1,2,0:T(8,128)(2,1)S(1)} async-done(((bf16[8,96,192]{1,2,0:T(8,128)(2,1)}), bf16[8,96,192]{1,2,0:T(8,128)(2,1)S(1)}, u32[]{:S(2)}, u32[]{:S(2)}) %all-to-all-start.2) | async-done | bytes 294944 | tf_op jit(solution)/shard_map/all_to_all | solution.py:215
  244.9 3.6 %all-to-all-start.4 = ((bf16[8,96,768]{2,1,0:T(8,128)(2,1)}), bf16[8,96,768]{2,1,0:T(8,128)(2,1)S(1)}, u32[]{:S(2)}, u32[]{:S(2)}) async-start(bf16[8,96,768]{2,1,0:T(8,128)(2,1)} %bitcast.61), calls=%async_computation.4 | async-start | bytes 2359296 | tf_op jit(solution)/shard_map/all_to_all | solution.py:215
  248.5 3.0 convolution_convert_fusion.1
  251.5 25.4 %all-to-all-done.4 = bf16[8,96,768]{2,1,0:T(8,128)(2,1)S(1)} async-done(((bf16[8,96,768]{2,1,0:T(8,128)(2,1)}), bf16[8,96,768]{2,1,0:T(8,128)(2,1)S(1)}, u32[]{:S(2)}, u32[]{:S(2)}) %all-to-all-start.4) | async-done | bytes 1179680 | tf_op jit(solution)/shard_map/all_to_all | solution.py:215
  276.9 3.6 %all-to-all-start.3 = ((bf16[8,96,768]{2,1,0:T(8,128)(2,1)}), bf16[8,96,768]{2,1,0:T(8,128)(2,1)S(1)}, u32[]{:S(2)}, u32[]{:S(2)}) async-start(bf16[8,96,768]{2,1,0:T(8,128)(2,1)} %bitcast.59), calls=%async_computation.3 | async-start | bytes 2359296 | tf_op jit(solution)/shard_map/all_to_all | solution.py:215
  280.5 8.7 %all_gather.29 = bf16[512,768]{1,0:T(8,128)(2,1)} all-gather(bf16[128,768]{1,0:T(8,128)(2,1)S(1)} %get-tuple-element.45), channel_id=1, replica_groups=mesh['dp'=8,'tp'=4] {'tp'}, dimensions={0}, use_global_device_ids=true | all-gather | bytes 983040 | tf_op jit(solution)/shard_map/all_gather | solution.py:235
  289.1 9.4 %all_gather.33 = bf16[512,768]{1,0:T(8,128)(2,1)} all-gather(bf16[128,768]{1,0:T(8,128)(2,1)S(1)} %get-tuple-element.44), channel_id=1, replica_groups=mesh['dp'=8,'tp'=4] {'tp'}, dimensions={0}, use_global_device_ids=true | all-gather | bytes 983040 | tf_op jit(solution)/shard_map/all_gather | solution.py:235
  298.6 1.7 convolution_convert_fusion.5
  300.3 1.8 dynamic-slice_bitcast_fusion
  303.9 2.2 copy.175
  306.2 5.3 %all-gather.1 = f32[4,36,128]{2,1,0:T(8,128)S(1)} all-gather(f32[1,36,128]{2,1,0:T(8,128)S(1)} %slice_bitcast_fusion.3), channel_id=2, replica_groups=mesh['dp'=8,'tp'=4] {'tp'}, dimensions={0}, use_global_device_ids=true | all-gather | bytes 92160 | tf_op jit(solution)/shard_map/all_gather | solution.py:230
  312.7 5.8 %all-to-all-start = ((bf16[8,96,576]{2,1,0:T(8,128)(2,1)}), bf16[8,96,576]{2,1,0:T(8,128)(2,1)S(1)}, u32[]{:S(2)}, u32[]{:S(2)}) async-start(bf16[8,96,576]{2,1,0:T(8,128)(2,1)} %bitcast.51), calls=%async_computation | async-start | bytes 1966080 | tf_op jit(solution)/shard_map/all_to_all | solution.py:215
  322.4 4.4 %collective-permute-done.35 = bf16[1,1,128,768]{3,2,1,0:T(8,128)(2,1)S(1)} collective-permute-done((bf16[1,1,128,768]{3,2,1,0:T(8,128)(2,1)S(1)}, bf16[1,1,128,768]{3,2,1,0:T(8,128)(2,1)S(1)}, u32[]{:S(2)}, u32[]{:S(2)}) %collective-permute-start.35) | collective-permute-done | bytes 196640 | tf_op jit(solution)/shard_map/ppermute | solution.py:66
  326.9 8.8 %all_gather.32 = bf16[512,768]{1,0:T(8,128)(2,1)} all-gather(bf16[128,768]{1,0:T(8,128)(2,1)S(1)} %fusion.57), channel_id=1, replica_groups=mesh['dp'=8,'tp'=4] {'tp'}, dimensions={0}, use_global_device_ids=true | all-gather | bytes 983040 | tf_op jit(solution)/shard_map/all_gather | solution.py:235
  337.4 6.0 %all-to-all-done = bf16[8,96,576]{2,1,0:T(8,128)(2,1)S(1)} async-done(((bf16[8,96,576]{2,1,0:T(8,128)(2,1)}), bf16[8,96,576]{2,1,0:T(8,128)(2,1)S(1)}, u32[]{:S(2)}, u32[]{:S(2)}) %all-to-all-start) | async-done | bytes 884768 | tf_op jit(solution)/shard_map/all_to_all | solution.py:215
  (288 shorter events, 71.3 us)
Async XLA Ops:
  0.7 5.5 %copy-start.33 = (bf16[192,96]{1,0:T(8,128)(2,1)S(1)}, bf16[192,96]{1,0:T(8,128)(2,1)}, u32[]{:S(2)}) copy-start(bf16[192,96]{1,0:T(8,128)(2,1)} %param.53) | copy-start | bytes 110596
  0.7 7.6 %copy-start.35 = (bf16[96,192]{1,0:T(8,128)(2,1)S(1)}, bf16[96,192]{1,0:T(8,128)(2,1)}, u32[]{:S(2)}) copy-start(bf16[96,192]{1,0:T(8,128)(2,1)} %param.34) | copy-start | bytes 110596
  0.7 7.6 %copy-start.36 = (bf16[96,192]{1,0:T(8,128)(2,1)S(1)}, bf16[96,192]{1,0:T(8,128)(2,1)}, u32[]{:S(2)}) copy-start(bf16[96,192]{1,0:T(8,128)(2,1)} %param.36) | copy-start | bytes 110596
  0.7 7.6 %copy-start.37 = (bf16[96,192]{1,0:T(8,128)(2,1)S(1)}, bf16[96,192]{1,0:T(8,128)(2,1)}, u32[]{:S(2)}) copy-start(bf16[96,192]{1,0:T(8,128)(2,1)} %param.37) | copy-start | bytes 110596
  0.7 7.6 %copy-start.38 = (bf16[96,192]{1,0:T(8,128)(2,1)S(1)}, bf16[96,192]{1,0:T(8,128)(2,1)}, u32[]{:S(2)}) copy-start(bf16[96,192]{1,0:T(8,128)(2,1)} %param.50) | copy-start | bytes 110596
  0.7 7.6 %copy-start.39 = (bf16[96,192]{1,0:T(8,128)(2,1)S(1)}, bf16[96,192]{1,0:T(8,128)(2,1)}, u32[]{:S(2)}) copy-start(bf16[96,192]{1,0:T(8,128)(2,1)} %param.51) | copy-start | bytes 110596
  0.8 7.6 %copy-start.40 = (bf16[96,192]{1,0:T(8,128)(2,1)S(1)}, bf16[96,192]{1,0:T(8,128)(2,1)}, u32[]{:S(2)}) copy-start(bf16[96,192]{1,0:T(8,128)(2,1)} %param.52) | copy-start | bytes 110596
  0.8 9.8 %copy-start.28 = (bf16[96,768]{1,0:T(8,128)(2,1)S(1)}, bf16[96,768]{1,0:T(8,128)(2,1)}, u32[]{:S(2)}) copy-start(bf16[96,768]{1,0:T(8,128)(2,1)} %param.43) | copy-start | bytes 442372
  3.2 48.0 %collective-permute-start.23 = (bf16[96,1536]{1,0:T(8,128)(2,1)S(1)}, bf16[96,1536]{1,0:T(8,128)(2,1)}, u32[]{:S(2)}, u32[]{:S(2)}) collective-permute-start(bf16[96,1536]{1,0:T(8,128)(2,1)S(1)} %get-tuple-element.47), channel_id=1, source_target_pairs={{0,8},{8,16},{16,24},{24,28},{28,20},{20,12},{12,4},{4,0},{1,9},{9... | collective-permute-start | bytes 884744 | tf_op jit(solution)/shard_map/ppermute | solution.py:44
  6.2 46.8 %collective-permute-start.24 = (bf16[96,1536]{1,0:T(8,128)(2,1)S(1)}, bf16[96,1536]{1,0:T(8,128)(2,1)}, u32[]{:S(2)}, u32[]{:S(2)}) collective-permute-start(bf16[96,1536]{1,0:T(8,128)(2,1)S(1)} %get-tuple-element.47), channel_id=1, source_target_pairs={{8,0},{16,8},{24,16},{28,24},{20,28},{12,20},{4,12},{0,4},{9,1},{1... | collective-permute-start | bytes 884744 | tf_op jit(solution)/shard_map/ppermute | solution.py:48
  6.2 9.9 %collective-permute-start.7 = (bf16[96,384]{0,1:T(8,128)(2,1)S(1)}, bf16[96,384]{0,1:T(8,128)(2,1)}, u32[]{:S(2)}, u32[]{:S(2)}) collective-permute-start(bf16[96,384]{0,1:T(8,128)(2,1)S(1)} %pad_maximum_fusion.1), channel_id=1, source_target_pairs={{0,8},{8,16},{16,24},{24,28},{28,20},{20,12},{12,4},{4,0},{1,9},{9... | collective-permute-start | bytes 221192 | tf_op jit(solution)/shard_map/ppermute | solution.py:44
  8.3 10.0 %collective-permute-start.8 = (bf16[96,384]{0,1:T(8,128)(2,1)S(1)}, bf16[96,384]{0,1:T(8,128)(2,1)}, u32[]{:S(2)}, u32[]{:S(2)}) collective-permute-start(bf16[96,384]{0,1:T(8,128)(2,1)S(1)} %pad_maximum_fusion.1), channel_id=1, source_target_pairs={{8,0},{16,8},{24,16},{28,24},{20,28},{12,20},{4,12},{0,4},{9,1},{1... | collective-permute-start | bytes 221192 | tf_op jit(solution)/shard_map/ppermute | solution.py:48
  8.5 28.9 %collective-permute-start = (bf16[96,1152]{1,0:T(8,128)(2,1)S(1)}, bf16[96,1152]{1,0:T(8,128)(2,1)S(1)}, u32[]{:S(2)}, u32[]{:S(2)}) collective-permute-start(bf16[96,1152]{1,0:T(8,128)(2,1)S(1)} %concatenate.26), channel_id=1, source_target_pairs={{0,8},{8,16},{16,24},{24,28},{28,20},{20,12},{12,4},{4,0},{1,9},{9... | collective-permute-start | bytes 663560 | tf_op jit(solution)/shard_map/ppermute | solution.py:44
  10.7 7.5 %copy-start.50 = (s32[2]{0:T(128)S(1)}, s32[2]{0:T(128)}, u32[]{:S(2)}) copy-start(s32[2]{0:T(128)} %param.33) | copy-start | bytes 28
  10.7 7.6 %copy-start.51 = (s32[8]{0:T(128)S(1)}, s32[8]{0:T(128)}, u32[]{:S(2)}) copy-start(s32[8]{0:T(128)} %constant.368.clone) | copy-start | bytes 100
  10.8 12.8 %copy-start.43 = (s32[8]{0:T(128)S(1)}, s32[8]{0:T(128)}, u32[]{:S(2)}) copy-start(s32[8]{0:T(128)} %constant.369.clone) | copy-start | bytes 100
  10.8 18.6 %copy-start.47 = (f32[192]{0:T(256)S(1)}, f32[192]{0:T(256)}, u32[]{:S(2)}) copy-start(f32[192]{0:T(256)} %param.35) | copy-start | bytes 2308
  10.8 18.6 %copy-start.48 = (f32[192]{0:T(256)S(1)}, f32[192]{0:T(256)}, u32[]{:S(2)}) copy-start(f32[192]{0:T(256)} %param.38) | copy-start | bytes 2308
  16.1 16.4 %collective-permute-start.9 = (bf16[96,384]{0,1:T(8,128)(2,1)}, bf16[96,384]{0,1:T(8,128)(2,1)}, u32[]{:S(2)}, u32[]{:S(2)}) collective-permute-start(bf16[96,384]{0,1:T(8,128)(2,1)} %collective-permute-done.7), channel_id=1, source_target_pairs={{0,8},{8,16},{16,24},{24,28},{28,20},{20,12},{12,4},{4,0},{1,9},{9... | collective-permute-start | bytes 221192 | tf_op jit(solution)/shard_map/ppermute | solution.py:44
  18.3 17.5 %collective-permute-start.10 = (bf16[96,384]{0,1:T(8,128)(2,1)}, bf16[96,384]{0,1:T(8,128)(2,1)}, u32[]{:S(2)}, u32[]{:S(2)}) collective-permute-start(bf16[96,384]{0,1:T(8,128)(2,1)} %collective-permute-done.8), channel_id=1, source_target_pairs={{8,0},{16,8},{24,16},{28,24},{20,28},{12,20},{4,12},{0,4},{9,1},{1... | collective-permute-start | bytes 221192 | tf_op jit(solution)/shard_map/ppermute | solution.py:48
  32.6 28.6 %collective-permute-start.16 = (bf16[96,1536]{1,0:T(8,128)(2,1)S(1)}, bf16[96,1536]{1,0:T(8,128)(2,1)}, u32[]{:S(2)}, u32[]{:S(2)}) collective-permute-start(bf16[96,1536]{1,0:T(8,128)(2,1)S(1)} %constant_dynamic-update-slice_fusion), channel_id=1, source_target_pairs={{0,8},{8,16},{16,24},{24,28},{28,20},{20,12},{12,4},{4,0},{1,9},{9... | collective-permute-start | bytes 884744 | tf_op jit(solution)/shard_map/ppermute | solution.py:44
  35.8 6.8 %collective-permute-start.1 = (bf16[96,1152]{1,0:T(8,128)(2,1)S(1)}, bf16[96,1152]{1,0:T(8,128)(2,1)}, u32[]{:S(2)}, u32[]{:S(2)}) collective-permute-start(bf16[96,1152]{1,0:T(8,128)(2,1)S(1)} %concatenate.26), channel_id=1, source_target_pairs={{8,0},{16,8},{24,16},{28,24},{20,28},{12,20},{4,12},{0,4},{9,1},{1... | collective-permute-start | bytes 663560 | tf_op jit(solution)/shard_map/ppermute | solution.py:48
  37.4 6.2 %collective-permute-start.11 = (bf16[96,384]{0,1:T(8,128)(2,1)}, bf16[96,384]{0,1:T(8,128)(2,1)S(1)}, u32[]{:S(2)}, u32[]{:S(2)}) collective-permute-start(bf16[96,384]{0,1:T(8,128)(2,1)} %collective-permute-done.9), channel_id=1, source_target_pairs={{0,8},{8,16},{16,24},{24,28},{28,20},{20,12},{12,4},{4,0},{1,9},{9... | collective-permute-start | bytes 221192 | tf_op jit(solution)/shard_map/ppermute | solution.py:44
  42.6 5.0 %collective-permute-start.12 = (bf16[96,384]{0,1:T(8,128)(2,1)}, bf16[96,384]{0,1:T(8,128)(2,1)}, u32[]{:S(2)}, u32[]{:S(2)}) collective-permute-start(bf16[96,384]{0,1:T(8,128)(2,1)} %collective-permute-done.10), channel_id=1, source_target_pairs={{8,0},{16,8},{24,16},{28,24},{20,28},{12,20},{4,12},{0,4},{9,1},{1... | collective-permute-start | bytes 221192 | tf_op jit(solution)/shard_map/ppermute | solution.py:48
  43.6 19.6 %collective-permute-start.17 = (bf16[96,1536]{1,0:T(8,128)(2,1)S(1)}, bf16[96,1536]{1,0:T(8,128)(2,1)}, u32[]{:S(2)}, u32[]{:S(2)}) collective-permute-start(bf16[96,1536]{1,0:T(8,128)(2,1)S(1)} %constant_dynamic-update-slice_fusion), channel_id=1, source_target_pairs={{8,0},{16,8},{24,16},{28,24},{20,28},{12,20},{4,12},{0,4},{9,1},{1... | collective-permute-start | bytes 884744 | tf_op jit(solution)/shard_map/ppermute | solution.py:48
  47.6 19.0 %collective-permute-start.2 = (bf16[96,1152]{1,0:T(8,128)(2,1)S(1)}, bf16[96,1152]{1,0:T(8,128)(2,1)S(1)}, u32[]{:S(2)}, u32[]{:S(2)}) collective-permute-start(bf16[96,1152]{1,0:T(8,128)(2,1)S(1)} %collective-permute-done), channel_id=1, source_target_pairs={{0,8},{8,16},{16,24},{24,28},{28,20},{20,12},{12,4},{4,0},{1,9},{9... | collective-permute-start | bytes 663560 | tf_op jit(solution)/shard_map/ppermute | solution.py:44
  51.2 15.8 %collective-permute-start.3 = (bf16[96,1152]{1,0:T(8,128)(2,1)}, bf16[96,1152]{1,0:T(8,128)(2,1)}, u32[]{:S(2)}, u32[]{:S(2)}) collective-permute-start(bf16[96,1152]{1,0:T(8,128)(2,1)} %collective-permute-done.1), channel_id=1, source_target_pairs={{8,0},{16,8},{24,16},{28,24},{20,28},{12,20},{4,12},{0,4},{9,1},{1... | collective-permute-start | bytes 663560 | tf_op jit(solution)/shard_map/ppermute | solution.py:48
  53.0 5.7 %collective-permute-start.13 = (bf16[96,384]{0,1:T(8,128)(2,1)S(1)}, bf16[96,384]{0,1:T(8,128)(2,1)S(1)}, u32[]{:S(2)}, u32[]{:S(2)}) collective-permute-start(bf16[96,384]{0,1:T(8,128)(2,1)S(1)} %collective-permute-done.11), channel_id=1, source_target_pairs={{0,8},{8,16},{16,24},{24,28},{28,20},{20,12},{12,4},{4,0},{1,9},{9... | collective-permute-start | bytes 221192 | tf_op jit(solution)/shard_map/ppermute | solution.py:44
  58.7 11.1 %collective-permute-start.25 = (bf16[96,1536]{1,0:T(8,128)(2,1)}, bf16[96,1536]{1,0:T(8,128)(2,1)}, u32[]{:S(2)}, u32[]{:S(2)}) collective-permute-start(bf16[96,1536]{1,0:T(8,128)(2,1)} %collective-permute-done.23), channel_id=1, source_target_pairs={{0,8},{8,16},{16,24},{24,28},{28,20},{20,12},{12,4},{4,0},{1,9},{9... | collective-permute-start | bytes 884744 | tf_op jit(solution)/shard_map/ppermute | solution.py:44
  61.2 17.3 %collective-permute-start.26 = (bf16[96,1536]{1,0:T(8,128)(2,1)}, bf16[96,1536]{1,0:T(8,128)(2,1)}, u32[]{:S(2)}, u32[]{:S(2)}) collective-permute-start(bf16[96,1536]{1,0:T(8,128)(2,1)} %collective-permute-done.24), channel_id=1, source_target_pairs={{8,0},{16,8},{24,16},{28,24},{20,28},{12,20},{4,12},{0,4},{9,1},{1... | collective-permute-start | bytes 884744 | tf_op jit(solution)/shard_map/ppermute | solution.py:48
  63.2 12.1 %collective-permute-start.18 = (bf16[96,1536]{1,0:T(8,128)(2,1)}, bf16[96,1536]{1,0:T(8,128)(2,1)}, u32[]{:S(2)}, u32[]{:S(2)}) collective-permute-start(bf16[96,1536]{1,0:T(8,128)(2,1)} %collective-permute-done.16), channel_id=1, source_target_pairs={{0,8},{8,16},{16,24},{24,28},{28,20},{20,12},{12,4},{4,0},{1,9},{9... | collective-permute-start | bytes 884744 | tf_op jit(solution)/shard_map/ppermute | solution.py:44
  66.7 15.7 %collective-permute-start.19 = (bf16[96,1536]{1,0:T(8,128)(2,1)}, bf16[96,1536]{1,0:T(8,128)(2,1)}, u32[]{:S(2)}, u32[]{:S(2)}) collective-permute-start(bf16[96,1536]{1,0:T(8,128)(2,1)} %collective-permute-done.17), channel_id=1, source_target_pairs={{8,0},{16,8},{24,16},{28,24},{20,28},{12,20},{4,12},{0,4},{9,1},{1... | collective-permute-start | bytes 884744 | tf_op jit(solution)/shard_map/ppermute | solution.py:48
  67.0 15.3 %collective-permute-start.4 = (bf16[96,1152]{1,0:T(8,128)(2,1)S(1)}, bf16[96,1152]{1,0:T(8,128)(2,1)S(1)}, u32[]{:S(2)}, u32[]{:S(2)}) collective-permute-start(bf16[96,1152]{1,0:T(8,128)(2,1)S(1)} %collective-permute-done.2), channel_id=1, source_target_pairs={{0,8},{8,16},{16,24},{24,28},{28,20},{20,12},{12,4},{4,0},{1,9},{9... | collective-permute-start | bytes 663560 | tf_op jit(solution)/shard_map/ppermute | solution.py:44
  69.7 21.0 %copy-start.19 = (bf16[512,768]{1,0:T(8,128)(2,1)S(1)}, bf16[512,768]{1,0:T(8,128)(2,1)}, u32[]{:S(2)}) copy-start(bf16[512,768]{1,0:T(8,128)(2,1)} %param.32) | copy-start | bytes 2359300
  69.7 13.0 %collective-permute-start.5 = (bf16[96,1152]{1,0:T(8,128)(2,1)}, bf16[96,1152]{1,0:T(8,128)(2,1)S(1)}, u32[]{:S(2)}, u32[]{:S(2)}) collective-permute-start(bf16[96,1152]{1,0:T(8,128)(2,1)} %collective-permute-done.3), channel_id=1, source_target_pairs={{8,0},{16,8},{24,16},{28,24},{20,28},{12,20},{4,12},{0,4},{9,1},{1... | collective-permute-start | bytes 663560 | tf_op jit(solution)/shard_map/ppermute | solution.py:48
  75.3 32.6 %collective-permute-start.27 = (bf16[96,1536]{1,0:T(8,128)(2,1)}, bf16[96,1536]{1,0:T(8,128)(2,1)}, u32[]{:S(2)}, u32[]{:S(2)}) collective-permute-start(bf16[96,1536]{1,0:T(8,128)(2,1)} %collective-permute-done.25), channel_id=1, source_target_pairs={{0,8},{8,16},{16,24},{24,28},{28,20},{20,12},{12,4},{4,0},{1,9},{9... | collective-permute-start | bytes 884744 | tf_op jit(solution)/shard_map/ppermute | solution.py:44
  78.4 32.5 %collective-permute-start.20 = (bf16[96,1536]{1,0:T(8,128)(2,1)}, bf16[96,1536]{1,0:T(8,128)(2,1)}, u32[]{:S(2)}, u32[]{:S(2)}) collective-permute-start(bf16[96,1536]{1,0:T(8,128)(2,1)} %collective-permute-done.18), channel_id=1, source_target_pairs={{0,8},{8,16},{16,24},{24,28},{28,20},{20,12},{12,4},{4,0},{1,9},{9... | collective-permute-start | bytes 884744 | tf_op jit(solution)/shard_map/ppermute | solution.py:44
  82.3 32.4 %collective-permute-start.28 = (bf16[96,1536]{1,0:T(8,128)(2,1)}, bf16[96,1536]{1,0:T(8,128)(2,1)}, u32[]{:S(2)}, u32[]{:S(2)}) collective-permute-start(bf16[96,1536]{1,0:T(8,128)(2,1)} %collective-permute-done.26), channel_id=1, source_target_pairs={{8,0},{16,8},{24,16},{28,24},{20,28},{12,20},{4,12},{0,4},{9,1},{1... | collective-permute-start | bytes 884744 | tf_op jit(solution)/shard_map/ppermute | solution.py:48
  82.3 32.3 %collective-permute-start.21 = (bf16[96,1536]{1,0:T(8,128)(2,1)}, bf16[96,1536]{1,0:T(8,128)(2,1)}, u32[]{:S(2)}, u32[]{:S(2)}) collective-permute-start(bf16[96,1536]{1,0:T(8,128)(2,1)} %collective-permute-done.19), channel_id=1, source_target_pairs={{8,0},{16,8},{24,16},{28,24},{20,28},{12,20},{4,12},{0,4},{9,1},{1... | collective-permute-start | bytes 884744 | tf_op jit(solution)/shard_map/ppermute | solution.py:48
  82.8 7.9 %collective-permute-start.6 = (bf16[96,1152]{1,0:T(8,128)(2,1)S(1)}, bf16[96,1152]{1,0:T(8,128)(2,1)S(1)}, u32[]{:S(2)}, u32[]{:S(2)}) collective-permute-start(bf16[96,1152]{1,0:T(8,128)(2,1)S(1)} %collective-permute-done.4), channel_id=1, source_target_pairs={{0,8},{8,16},{16,24},{24,28},{28,20},{20,12},{12,4},{4,0},{1,9},{9... | collective-permute-start | bytes 663560 | tf_op jit(solution)/shard_map/ppermute | solution.py:44
  106.0 10.6 %collective-permute-start.14 = (bf16[2,2,128,768]{3,2,1,0:T(8,128)(2,1)S(1)}, bf16[2,2,128,768]{3,2,1,0:T(8,128)(2,1)S(1)}, u32[]{:S(2)}, u32[]{:S(2)}) collective-permute-start(bf16[2,2,128,768]{3,2,1,0:T(8,128)(2,1)S(1)} %fusion.39), channel_id=1, source_target_pairs={{0,1},{1,0},{2,3},{3,2},{4,5},{5,4},{6,7},{7,6},{8,9},{9,8},{10,11... | collective-permute-start | bytes 2359304 | tf_op jit(solution)/shard_map/ppermute | solution.py:66
  107.8 16.7 %collective-permute-start.29 = (bf16[96,1536]{1,0:T(8,128)(2,1)}, bf16[96,1536]{1,0:T(8,128)(2,1)S(1)}, u32[]{:S(2)}, u32[]{:S(2)}) collective-permute-start(bf16[96,1536]{1,0:T(8,128)(2,1)} %collective-permute-done.27), channel_id=1, source_target_pairs={{0,8},{8,16},{16,24},{24,28},{28,20},{20,12},{12,4},{4,0},{1,9},{9... | collective-permute-start | bytes 884744 | tf_op jit(solution)/shard_map/ppermute | solution.py:44
  111.0 12.8 %collective-permute-start.22 = (bf16[96,1536]{1,0:T(8,128)(2,1)}, bf16[96,1536]{1,0:T(8,128)(2,1)S(1)}, u32[]{:S(2)}, u32[]{:S(2)}) collective-permute-start(bf16[96,1536]{1,0:T(8,128)(2,1)} %collective-permute-done.20), channel_id=1, source_target_pairs={{0,8},{8,16},{16,24},{24,28},{28,20},{20,12},{12,4},{4,0},{1,9},{9... | collective-permute-start | bytes 884744 | tf_op jit(solution)/shard_map/ppermute | solution.py:44
  116.8 11.0 %collective-permute-start.15 = (bf16[2,1,128,768]{3,2,1,0:T(8,128)(2,1)S(1)}, bf16[2,1,128,768]{3,2,1,0:T(8,128)(2,1)S(1)}, u32[]{:S(2)}, u32[]{:S(2)}) collective-permute-start(bf16[2,1,128,768]{3,2,1,0:T(8,128)(2,1)S(1)} %constant_dynamic-slice_fusion), channel_id=1, source_target_pairs={{0,2},{1,3},{2,0},{3,1},{4,6},{5,7},{6,4},{7,5},{8,10},{9,11},{10,... | collective-permute-start | bytes 1179656 | tf_op jit(solution)/shard_map/ppermute | solution.py:66
  164.4 2.4 collective-permute-start.30
  167.0 11.6 %copy-start.45 = (f32[768]{0:T(1024)S(1)}, f32[768]{0:T(1024)}, u32[]{:S(2)}) copy-start(f32[768]{0:T(1024)} %param.46) | copy-start | bytes 9220
  167.0 11.4 %collective-permute-start.31 = (bf16[2,1,128,768]{3,2,1,0:T(8,128)(2,1)S(1)}, bf16[2,1,128,768]{3,2,1,0:T(8,128)(2,1)S(1)}, u32[]{:S(2)}, u32[]{:S(2)}) collective-permute-start(bf16[2,1,128,768]{3,2,1,0:T(8,128)(2,1)S(1)} %constant_dynamic-slice_fusion.1), channel_id=1, source_target_pairs={{0,2},{1,3},{2,0},{3,1},{4,6},{5,7},{6,4},{7,5},{8,10},{9,11},{10,... | collective-permute-start | bytes 1179656 | tf_op jit(solution)/shard_map/ppermute | solution.py:66
  179.3 8.4 %copy-start.54 = (f32[512,768]{1,0:T(8,128)S(1)}, f32[512,768]{1,0:T(8,128)}, u32[]{:S(2)}) copy-start(f32[512,768]{1,0:T(8,128)} %get-tuple-element.72) | copy-start | bytes 4718596
  192.8 1.8 collective-permute-start.32
  194.7 7.2 %collective-permute-start.33 = (bf16[1,1,128,768]{3,2,1,0:T(8,128)(2,1)S(1)}, bf16[1,1,128,768]{3,2,1,0:T(8,128)(2,1)S(1)}, u32[]{:S(2)}, u32[]{:S(2)}) collective-permute-start(bf16[1,1,128,768]{3,2,1,0:T(8,128)(2,1)S(1)} %constant_dynamic-slice_fusion.2), channel_id=1, source_target_pairs={{0,2},{1,3},{2,0},{3,1},{4,6},{5,7},{6,4},{7,5},{8,10},{9,11},{10,... | collective-permute-start | bytes 589832 | tf_op jit(solution)/shard_map/ppermute | solution.py:66
  202.5 8.8 %copy-start = (f32[128,768]{1,0:T(8,128)}, f32[128,768]{1,0:T(8,128)S(1)}, u32[]{:S(2)}) copy-start(f32[128,768]{1,0:T(8,128)S(1)} %get-tuple-element.28) | copy-start | bytes 1179652
  217.0 12.1 %all-to-all-start.1 = ((f32[8,47,128]{2,1,0:T(8,128)}), f32[8,47,128]{2,1,0:T(8,128)S(1)}, u32[]{:S(2)}, u32[]{:S(2)}) async-start(f32[8,47,128]{2,1,0:T(8,128)} %broadcast_in_dim.38), calls=%async_computation.1 | async-start | bytes 393216 | tf_op jit(solution)/shard_map/all_to_all | solution.py:227
  220.4 12.1 %copy-start.18 = (bf16[512,768]{1,0:T(8,128)(2,1)S(1)}, bf16[512,768]{1,0:T(8,128)(2,1)}, u32[]{:S(2)}) copy-start(bf16[512,768]{1,0:T(8,128)(2,1)} %copy-done.17) | copy-start | bytes 2359300
  229.1 15.0 %all-to-all-start.2 = ((bf16[8,96,192]{1,2,0:T(8,128)(2,1)}), bf16[8,96,192]{1,2,0:T(8,128)(2,1)S(1)}, u32[]{:S(2)}, u32[]{:S(2)}) async-start(bf16[8,96,192]{1,2,0:T(8,128)(2,1)} %copy.177), calls=%async_computation.2 | async-start | bytes 786432 | tf_op jit(solution)/shard_map/all_to_all | solution.py:215
  235.6 12.9 %copy-start.16 = (bf16[512,768]{1,0:T(8,128)(2,1)S(1)}, bf16[512,768]{1,0:T(8,128)(2,1)}, u32[]{:S(2)}) copy-start(bf16[512,768]{1,0:T(8,128)(2,1)} %copy-done.15) | copy-start | bytes 2359300
  244.9 32.0 %all-to-all-start.4 = ((bf16[8,96,768]{2,1,0:T(8,128)(2,1)}), bf16[8,96,768]{2,1,0:T(8,128)(2,1)S(1)}, u32[]{:S(2)}, u32[]{:S(2)}) async-start(bf16[8,96,768]{2,1,0:T(8,128)(2,1)} %bitcast.61), calls=%async_computation.4 | async-start | bytes 2359296 | tf_op jit(solution)/shard_map/all_to_all | solution.py:215
  276.9 35.9 %all-to-all-start.3 = ((bf16[8,96,768]{2,1,0:T(8,128)(2,1)}), bf16[8,96,768]{2,1,0:T(8,128)(2,1)S(1)}, u32[]{:S(2)}, u32[]{:S(2)}) async-start(bf16[8,96,768]{2,1,0:T(8,128)(2,1)} %bitcast.59), calls=%async_computation.3 | async-start | bytes 2359296 | tf_op jit(solution)/shard_map/all_to_all | solution.py:215
  280.4 18.1 %copy-start.6 = (bf16[768,1152]{1,0:T(8,128)(2,1)S(1)}, bf16[768,1152]{1,0:T(8,128)(2,1)}, u32[]{:S(2)}) copy-start(bf16[768,1152]{1,0:T(8,128)(2,1)} %copy-done.5) | copy-start | bytes 5308420
  302.0 16.5 %collective-permute-start.34 = (bf16[1,2,128,768]{3,2,1,0:T(8,128)(2,1)}, bf16[1,2,128,768]{3,2,1,0:T(8,128)(2,1)}, u32[]{:S(2)}, u32[]{:S(2)}) collective-permute-start(bf16[1,2,128,768]{3,2,1,0:T(8,128)(2,1)} %dynamic-slice_bitcast_fusion), channel_id=1, source_target_pairs={{0,1},{1,0},{2,3},{3,2},{4,5},{5,4},{6,7},{7,6},{8,9},{9,8},{10,11... | collective-permute-start | bytes 1179656 | tf_op jit(solution)/shard_map/ppermute | solution.py:66
  312.7 30.7 %all-to-all-start = ((bf16[8,96,576]{2,1,0:T(8,128)(2,1)}), bf16[8,96,576]{2,1,0:T(8,128)(2,1)S(1)}, u32[]{:S(2)}, u32[]{:S(2)}) async-start(bf16[8,96,576]{2,1,0:T(8,128)(2,1)} %bitcast.51), calls=%async_computation | async-start | bytes 1966080 | tf_op jit(solution)/shard_map/all_to_all | solution.py:215
  318.5 8.3 %copy-start.1 = (f32[128,768]{1,0:T(8,128)S(1)}, f32[128,768]{1,0:T(8,128)}, u32[]{:S(2)}) copy-start(f32[128,768]{1,0:T(8,128)} %copy-done) | copy-start | bytes 1179652
  319.9 6.9 %collective-permute-start.35 = (bf16[1,1,128,768]{3,2,1,0:T(8,128)(2,1)S(1)}, bf16[1,1,128,768]{3,2,1,0:T(8,128)(2,1)S(1)}, u32[]{:S(2)}, u32[]{:S(2)}) collective-permute-start(bf16[1,1,128,768]{3,2,1,0:T(8,128)(2,1)S(1)} %constant_dynamic-slice_fusion.3), channel_id=1, source_target_pairs={{0,2},{1,3},{2,0},{3,1},{4,6},{5,7},{6,4},{7,5},{8,10},{9,11},{10,... | collective-permute-start | bytes 589832 | tf_op jit(solution)/shard_map/ppermute | solution.py:66
  336.5 7.8 %copy-start.3 = (bf16[512,768]{1,0:T(8,128)(2,1)S(1)}, bf16[512,768]{1,0:T(8,128)(2,1)}, u32[]{:S(2)}) copy-start(bf16[512,768]{1,0:T(8,128)(2,1)} %all_gather.29) | copy-start | bytes 2359300
  337.4 7.8 %copy-start.4 = (bf16[512,768]{1,0:T(8,128)(2,1)S(1)}, bf16[512,768]{1,0:T(8,128)(2,1)}, u32[]{:S(2)}) copy-start(bf16[512,768]{1,0:T(8,128)(2,1)} %all_gather.32) | copy-start | bytes 2359300
  (32 other events, 80.3 us)
where the time goes:
time: 349 us; the launch traced here: 347 us
  waiting for transfers between devices  98.1 us (28%)
  blocking collectives  66.5 us (19%)
  starting transfers between devices  61.3 us (18%)
  local copies, waits for them, and re-layouts  57.4 us (16%)
  matrix products  43.8 us (13%)
  between operations  11.3 us (3%)
  other arithmetic  8.69 us (2%)
    all_to_all x4, waiting for transfers between devices, spread(): came = lax.all_to_all(split, 'dp', 0, 0, tiled=True)  40 us
    dot_general x17, matrix products, dot(): lax.dot_general(left, right, (dims, ((), ())), preferred_element_type=F32)  35.7 us
    ppermute x16, starting transfers between devices, gather_rows(): one = lax.ppermute(one, 'dp', ahead)  31.3 us
    ppermute x8, waiting for transfers between devices, scatter_sum(): came = lax.ppermute(send.astype(BF), 'tp', xor_pairs(tp, bit))  27 us
    all_gather x3, blocking collectives, all_rows(): return lax.all_gather(block, 'tp', axis=0, tiled=True)  26.9 us
    ppermute x16, waiting for transfers between devices, gather_rows(): one = lax.ppermute(one, 'dp', ahead)  19.9 us
    all_to_all x4, starting transfers between devices, spread(): came = lax.all_to_all(split, 'dp', 0, 0, tiled=True)  16.4 us
    dynamic_update_slice x16, local copies, waits for them, and re-layouts, gather_rows(): whole = lax.dynamic_update_slice(whole, one, (owner * rows, 0))  16.2 us
  transfers between devices with their start and end apart: 41, of which 17 were waited for; matrix products, arithmetic and copies ran while one was open for 20% of the time, Pallas kernels for 0%

commit v1 on v0

--- a/solution.py
+++ b/solution.py
@@ -192,7 +192,17 @@
     shift_one = jnp.sum(grad_first, axis=0)
     grad_one = norm_along(unit_one, inverse_one, grad_first * first_gain)
     bias_out = jnp.sum(grad_one, axis=0)
-    grad_attn = lax.all_gather(grad_one.astype(BF), "tp", axis=0, tiled=True)
+    x = grad_one.astype(BF)
+    ways = lax.axis_size("tp")
+    up = [(d, (d + 1) % ways) for d in range(ways)]
+    down = [(d, (d - 1) % ways) for d in range(ways)]
+    earlier, later = ([x], [x])
+    for _ in range(ways // 2):
+        earlier.append(lax.ppermute(earlier[-1], "tp", up))
+    for _ in range((ways - 1) // 2):
+        later.append(lax.ppermute(later[-1], "tp", down))
+    line = jnp.concatenate([*earlier[::-1], *later[1:]], axis=0)
+    grad_attn = jnp.roll(line, (lax.axis_index("tp") - ways // 2) * x.shape[0], axis=0)
     step_out = dot(grad_attn, context, TN).astype(BF)
     grad_context = dot(grad_attn, out_full, NN).astype(BF).reshape(pairs, SEQ, heads, HEAD)
     grad_values = ein("phqk,pqhd->pkhd", probs_low, grad_context).astype(BF)

time: 349 us -> 364 us (1.043)
  waiting for transfers between devices: 98.1 us -> 110 us
  blocking collectives: 66.5 us -> 58.1 us
  other arithmetic: 8.69 us -> 14.8 us
  local copies, waits for them, and re-layouts: 57.4 us -> 62.4 us
    ppermute x0 -> x3, waiting for transfers between devices: none -> 9.2 us  [the longest x2 8.96 us: per_device(): earlier.append(lax.ppermute(earlier[-1], 'tp', up))]
    all_gather x1 -> x0, blocking collectives: 8.32 us -> none  [per_device(): grad_attn = lax.all_gather(grad_one.astype(BF), 'tp', axis=0, tiled=True)]
    unnamed x122 -> x155, local copies, waits for them, and re-layouts: 5.83 us -> 9.74 us
    all_to_all x4, waiting for transfers between devices: 40 us -> 43.8 us  [spread(): came = lax.all_to_all(split, 'dp', 0, 0, tiled=True)]
  transfers between devices with their start and end apart: 41 -> 44, of which waited for: 17 -> 20; matrix products, arithmetic and copies ran while one was open for 20% -> 20% of each run, Pallas kernels for 0% -> 0%
where the time goes in v1:
time: 364 us; the launch traced here: 362 us
  waiting for transfers between devices  110 us (30%)
  starting transfers between devices  63 us (17%)
  local copies, waits for them, and re-layouts  62.4 us (17%)
  blocking collectives  58.1 us (16%)
  matrix products  41.4 us (11%)
  other arithmetic  14.8 us (4%)
  between operations  11.4 us (3%)
    all_to_all x4, waiting for transfers between devices, spread(): came = lax.all_to_all(split, 'dp', 0, 0, tiled=True)  43.8 us
    dot_general x17, matrix products, dot(): lax.dot_general(left, right, (dims, ((), ())), preferred_element_type=F32)  35.7 us
    ppermute x16, starting transfers between devices, gather_rows(): one = lax.ppermute(one, 'dp', ahead)  31.5 us
    ppermute x8, waiting for transfers between devices, scatter_sum(): came = lax.ppermute(send.astype(BF), 'tp', xor_pairs(tp, bit))  27.4 us
    all_gather x3, blocking collectives, all_rows(): return lax.all_gather(block, 'tp', axis=0, tiled=True)  26.5 us
    ppermute x16, waiting for transfers between devices, gather_rows(): one = lax.ppermute(one, 'dp', ahead)  19.8 us
    all_to_all x4, starting transfers between devices, spread(): came = lax.all_to_all(split, 'dp', 0, 0, tiled=True)  16.7 us
    dynamic_update_slice x16, local copies, waits for them, and re-layouts, gather_rows(): whole = lax.dynamic_update_slice(whole, one, (owner * rows, 0))  16.2 us
  transfers between devices with their start and end apart: 44, of which 20 were waited for; matrix products, arithmetic and copies ran while one was open for 20% of the time, Pallas kernels for 0%

profile of v1, /device:TPU:0, one launch (start us, length us, event | category | flops | bytes accessed | tf_op | source)
XLA Modules:
  0.0 361.5 jit_solution(10117962407216565816)
XLA Ops:
  3.1 3.0 collective-permute-start.23
  6.2 2.1 collective-permute-start.7
  8.5 2.1 collective-permute-start
  13.1 3.0 collective-permute-done.7
  16.1 2.1 collective-permute-start.9
  32.6 1.7 collective-permute-start.16
  37.4 2.1 collective-permute-start.11
  39.5 3.1 collective-permute-done.1
  43.6 2.2 collective-permute-start.17
  47.6 2.0 collective-permute-start.2
  53.0 2.0 collective-permute-start.13
  56.7 2.0 collective-permute-done.13
  58.7 1.8 collective-permute-start.25
  63.2 1.7 collective-permute-start.18
  67.0 1.8 collective-permute-start.4
  71.8 3.5 collective-permute-done.18
  78.4 2.3 collective-permute-start.20
  82.8 2.0 collective-permute-start.6
  84.8 5.9 %collective-permute-done.6 = bf16[96,1152]{1,0:T(8,128)(2,1)S(1)} collective-permute-done((bf16[96,1152]{1,0:T(8,128)(2,1)S(1)}, bf16[96,1152]{1,0:T(8,128)(2,1)S(1)}, u32[]{:S(2)}, u32[]{:S(2)}) %collective-permute-start.6) | collective-permute-done | bytes 221216 | tf_op jit(solution)/shard_map/ppermute | solution.py:44
  90.7 2.2 fusion.2
  92.9 2.9 reshape.362
  95.9 1.7 fusion.91
  97.6 1.7 fusion.95
  105.4 1.7 constant_dynamic-update-slice_fusion.19
  108.5 1.7 constant_dynamic-update-slice_fusion.17
  110.2 2.0 collective-permute-start.22
  112.2 1.7 constant_dynamic-update-slice_fusion.14
  113.9 1.9 constant_dynamic-update-slice_fusion.15
  117.6 5.4 %collective-permute-done.22 = bf16[96,1536]{1,0:T(8,128)(2,1)S(1)} collective-permute-done((bf16[96,1536]{1,0:T(8,128)(2,1)}, bf16[96,1536]{1,0:T(8,128)(2,1)S(1)}, u32[]{:S(2)}, u32[]{:S(2)}) %collective-permute-start.22) | collective-permute-done | bytes 294944 | tf_op jit(solution)/shard_map/ppermute | solution.py:44
  124.5 2.5 collective-permute-done.15
  128.1 8.6 %all_gather.24 = bf16[512,768]{1,0:T(8,128)(2,1)S(1)} all-gather(bf16[128,768]{1,0:T(8,128)(2,1)S(1)} %get-tuple-element.46), channel_id=1, replica_groups=mesh['dp'=8,'tp'=4] {'tp'}, dimensions={0}, use_global_device_ids=true | all-gather | bytes 983040 | tf_op jit(solution)/shard_map/all_gather | solution.py:163
  136.7 3.5 fusion.14
  140.2 3.3 multiply_convert_fusion.2
  143.5 3.6 fusion.12
  147.1 2.1 convolution_convert_fusion.4
  149.2 9.4 %all_gather.25 = bf16[512,768]{1,0:T(8,128)(2,1)} all-gather(bf16[128,768]{1,0:T(8,128)(2,1)S(1)} %get-tuple-element.33), channel_id=1, replica_groups=mesh['dp'=8,'tp'=4] {'tp'}, dimensions={0}, use_global_device_ids=true | all-gather | bytes 983040 | tf_op jit(solution)/shard_map/all_gather | solution.py:164
  158.6 4.9 %add_convert_fusion = bf16[512,768]{1,0:T(8,128)(2,1)S(1)} fusion(f32[512,768]{1,0:T(8,128)} %fusion.12, bf16[768,1536]{1,0:T(8,128)(2,1)} %constant_dynamic-update-slice_fusion.28, f32[512,768]{1,0:T(8,128)} %fusion.14, bf16[512,768]{1,0:T(8,128)(2,1)} %all_gather.25, bf16[768,1536]{1,0:T(8,128)(2,1)} %constant_dynamic-update-slice_fusion.24, ...), kind=kOutput, calls=%fused_computation.27 | convolution fusion | flops 1213071360 | bytes 8650752 | tf_op jit(solution)/shard_map/dot_general | solution.py:15
  164.0 1.9 collective-permute-done.30
  166.9 10.7 %collective-permute-done.31 = bf16[2,1,128,768]{3,2,1,0:T(8,128)(2,1)S(1)} collective-permute-done((bf16[2,1,128,768]{3,2,1,0:T(8,128)(2,1)S(1)}, bf16[2,1,128,768]{3,2,1,0:T(8,128)(2,1)S(1)}, u32[]{:S(2)}, u32[]{:S(2)}) %collective-permute-start.31) | collective-permute-done | bytes 393248 | tf_op jit(solution)/shard_map/ppermute | solution.py:66
  179.6 7.9 %all_gather.27 = bf16[512,768]{1,0:T(8,128)(2,1)S(1)} all-gather(bf16[128,768]{1,0:T(8,128)(2,1)S(1)} %convert_element_type.267), channel_id=1, replica_groups=mesh['dp'=8,'tp'=4] {'tp'}, dimensions={0}, use_global_device_ids=true | all-gather | bytes 983040 | tf_op jit(solution)/shard_map/all_gather | solution.py:181
  187.5 3.2 fusion.96
  190.7 2.4 convolution_convert_fusion.3
  196.4 5.9 %collective-permute-done.33 = bf16[1,1,128,768]{3,2,1,0:T(8,128)(2,1)S(1)} collective-permute-done((bf16[1,1,128,768]{3,2,1,0:T(8,128)(2,1)S(1)}, bf16[1,1,128,768]{3,2,1,0:T(8,128)(2,1)S(1)}, u32[]{:S(2)}, u32[]{:S(2)}) %collective-permute-start.33) | collective-permute-done | bytes 196640 | tf_op jit(solution)/shard_map/ppermute | solution.py:66
  204.0 5.1 %collective-permute-done.34 = bf16[128,768]{1,0:T(8,128)(2,1)S(1)} collective-permute-done((bf16[128,768]{1,0:T(8,128)(2,1)S(1)}, bf16[128,768]{1,0:T(8,128)(2,1)S(1)}, u32[]{:S(2)}, u32[]{:S(2)}) %collective-permute-start.34) | collective-permute-done | bytes 196640 | tf_op jit(solution)/shard_map/ppermute | solution.py:201
  209.1 1.7 collective-permute-start.36
  210.9 3.9 %collective-permute-done.35 = bf16[128,768]{1,0:T(8,128)(2,1)S(1)} collective-permute-done((bf16[128,768]{1,0:T(8,128)(2,1)S(1)}, bf16[128,768]{1,0:T(8,128)(2,1)S(1)}, u32[]{:S(2)}, u32[]{:S(2)}) %collective-permute-start.35) | collective-permute-done | bytes 196640 | tf_op jit(solution)/shard_map/ppermute | solution.py:201
  222.2 3.4 all-to-all-start.1
  228.5 6.1 %all-to-all-done.1 = f32[8,47,128]{2,1,0:T(8,128)S(1)} async-done(((f32[8,47,128]{2,1,0:T(8,128)}), f32[8,47,128]{2,1,0:T(8,128)S(1)}, u32[]{:S(2)}, u32[]{:S(2)}) %all-to-all-start.1) | async-done | bytes 192544 | tf_op jit(solution)/shard_map/all_to_all | solution.py:237
  234.5 3.5 all-to-all-start.2
  238.0 1.8 convolution_convert_fusion
  239.9 10.3 %all-to-all-done.2 = bf16[8,96,192]{1,2,0:T(8,128)(2,1)S(1)} async-done(((bf16[8,96,192]{1,2,0:T(8,128)(2,1)}), bf16[8,96,192]{1,2,0:T(8,128)(2,1)S(1)}, u32[]{:S(2)}, u32[]{:S(2)}) %all-to-all-start.2) | async-done | bytes 294944 | tf_op jit(solution)/shard_map/all_to_all | solution.py:225
  250.9 3.6 %all-to-all-start.4 = ((bf16[8,96,768]{2,1,0:T(8,128)(2,1)}), bf16[8,96,768]{2,1,0:T(8,128)(2,1)S(1)}, u32[]{:S(2)}, u32[]{:S(2)}) async-start(bf16[8,96,768]{2,1,0:T(8,128)(2,1)} %bitcast.61), calls=%async_computation.4 | async-start | bytes 2359296 | tf_op jit(solution)/shard_map/all_to_all | solution.py:225
  254.5 1.9 convolution_convert_fusion.1
  256.4 26.9 %all-to-all-done.4 = bf16[8,96,768]{2,1,0:T(8,128)(2,1)S(1)} async-done(((bf16[8,96,768]{2,1,0:T(8,128)(2,1)}), bf16[8,96,768]{2,1,0:T(8,128)(2,1)S(1)}, u32[]{:S(2)}, u32[]{:S(2)}) %all-to-all-start.4) | async-done | bytes 1179680 | tf_op jit(solution)/shard_map/all_to_all | solution.py:225
  283.3 3.6 %all-to-all-start.3 = ((bf16[8,96,768]{2,1,0:T(8,128)(2,1)}), bf16[8,96,768]{2,1,0:T(8,128)(2,1)S(1)}, u32[]{:S(2)}, u32[]{:S(2)}) async-start(bf16[8,96,768]{2,1,0:T(8,128)(2,1)} %bitcast.249), calls=%async_computation.3 | async-start | bytes 2359296 | tf_op jit(solution)/shard_map/all_to_all | solution.py:225
  286.9 9.0 %all_gather.26 = bf16[512,768]{1,0:T(8,128)(2,1)} all-gather(bf16[128,768]{1,0:T(8,128)(2,1)S(1)} %copy-done.22), channel_id=1, replica_groups=mesh['dp'=8,'tp'=4] {'tp'}, dimensions={0}, use_global_device_ids=true | all-gather | bytes 983040 | tf_op jit(solution)/shard_map/all_gather | solution.py:245
  295.9 9.2 %all_gather.29 = bf16[512,768]{1,0:T(8,128)(2,1)S(1)} all-gather(bf16[128,768]{1,0:T(8,128)(2,1)} %get-tuple-element.44), channel_id=1, replica_groups=mesh['dp'=8,'tp'=4] {'tp'}, dimensions={0}, use_global_device_ids=true | all-gather | bytes 983040 | tf_op jit(solution)/shard_map/all_gather | solution.py:245
  305.1 2.0 convolution_convert_fusion.5
  310.7 2.2 copy.175
  315.2 5.7 %all-gather.1 = f32[4,36,128]{2,1,0:T(8,128)} all-gather(f32[1,36,128]{2,1,0:T(8,128)S(1)} %slice_bitcast_fusion.3), channel_id=2, replica_groups=mesh['dp'=8,'tp'=4] {'tp'}, dimensions={0}, use_global_device_ids=true | all-gather | bytes 92160 | tf_op jit(solution)/shard_map/all_gather | solution.py:240
  325.8 6.0 %all-to-all-start = ((bf16[8,96,576]{2,1,0:T(8,128)(2,1)}), bf16[8,96,576]{2,1,0:T(8,128)(2,1)}, u32[]{:S(2)}, u32[]{:S(2)}) async-start(bf16[8,96,576]{2,1,0:T(8,128)(2,1)} %bitcast.241), calls=%async_computation | async-start | bytes 1966080 | tf_op jit(solution)/shard_map/all_to_all | solution.py:225
  335.2 4.9 %collective-permute-done.38 = bf16[1,1,128,768]{3,2,1,0:T(8,128)(2,1)S(1)} collective-permute-done((bf16[1,1,128,768]{3,2,1,0:T(8,128)(2,1)S(1)}, bf16[1,1,128,768]{3,2,1,0:T(8,128)(2,1)S(1)}, u32[]{:S(2)}, u32[]{:S(2)}) %collective-permute-start.38) | collective-permute-done | bytes 196640 | tf_op jit(solution)/shard_map/ppermute | solution.py:66
  340.1 8.3 %all_gather.28 = bf16[512,768]{1,0:T(8,128)(2,1)} all-gather(bf16[128,768]{1,0:T(8,128)(2,1)S(1)} %fusion.59), channel_id=1, replica_groups=mesh['dp'=8,'tp'=4] {'tp'}, dimensions={0}, use_global_device_ids=true | all-gather | bytes 983040 | tf_op jit(solution)/shard_map/all_gather | solution.py:245
  350.1 6.6 %all-to-all-done = bf16[8,96,576]{2,1,0:T(8,128)(2,1)} async-done(((bf16[8,96,576]{2,1,0:T(8,128)(2,1)}), bf16[8,96,576]{2,1,0:T(8,128)(2,1)}, u32[]{:S(2)}, u32[]{:S(2)}) %all-to-all-start) | async-done | bytes 884768 | tf_op jit(solution)/shard_map/all_to_all | solution.py:225
  (329 shorter events, 85.0 us)
Async XLA Ops:
  0.7 7.6 %copy-start.39 = (bf16[96,192]{1,0:T(8,128)(2,1)S(1)}, bf16[96,192]{1,0:T(8,128)(2,1)}, u32[]{:S(2)}) copy-start(bf16[96,192]{1,0:T(8,128)(2,1)} %param.34) | copy-start | bytes 110596
  0.7 7.6 %copy-start.40 = (bf16[96,192]{1,0:T(8,128)(2,1)S(1)}, bf16[96,192]{1,0:T(8,128)(2,1)}, u32[]{:S(2)}) copy-start(bf16[96,192]{1,0:T(8,128)(2,1)} %param.36) | copy-start | bytes 110596
  0.8 9.8 %copy-start.32 = (bf16[96,768]{1,0:T(8,128)(2,1)S(1)}, bf16[96,768]{1,0:T(8,128)(2,1)}, u32[]{:S(2)}) copy-start(bf16[96,768]{1,0:T(8,128)(2,1)} %param.43) | copy-start | bytes 442372
  3.1 48.1 %collective-permute-start.23 = (bf16[96,1536]{1,0:T(8,128)(2,1)S(1)}, bf16[96,1536]{1,0:T(8,128)(2,1)}, u32[]{:S(2)}, u32[]{:S(2)}) collective-permute-start(bf16[96,1536]{1,0:T(8,128)(2,1)S(1)} %get-tuple-element.47), channel_id=1, source_target_pairs={{0,8},{8,16},{16,24},{24,28},{28,20},{20,12},{12,4},{4,0},{1,9},{9... | collective-permute-start | bytes 884744 | tf_op jit(solution)/shard_map/ppermute | solution.py:44
  6.1 46.8 %collective-permute-start.24 = (bf16[96,1536]{1,0:T(8,128)(2,1)S(1)}, bf16[96,1536]{1,0:T(8,128)(2,1)}, u32[]{:S(2)}, u32[]{:S(2)}) collective-permute-start(bf16[96,1536]{1,0:T(8,128)(2,1)S(1)} %get-tuple-element.47), channel_id=1, source_target_pairs={{8,0},{16,8},{24,16},{28,24},{20,28},{12,20},{4,12},{0,4},{9,1},{1... | collective-permute-start | bytes 884744 | tf_op jit(solution)/shard_map/ppermute | solution.py:48
  6.2 9.9 %collective-permute-start.7 = (bf16[96,384]{0,1:T(8,128)(2,1)S(1)}, bf16[96,384]{0,1:T(8,128)(2,1)}, u32[]{:S(2)}, u32[]{:S(2)}) collective-permute-start(bf16[96,384]{0,1:T(8,128)(2,1)S(1)} %pad_maximum_fusion.1), channel_id=1, source_target_pairs={{0,8},{8,16},{16,24},{24,28},{28,20},{20,12},{12,4},{4,0},{1,9},{9... | collective-permute-start | bytes 221192 | tf_op jit(solution)/shard_map/ppermute | solution.py:44
  8.3 10.0 %collective-permute-start.8 = (bf16[96,384]{0,1:T(8,128)(2,1)S(1)}, bf16[96,384]{0,1:T(8,128)(2,1)}, u32[]{:S(2)}, u32[]{:S(2)}) collective-permute-start(bf16[96,384]{0,1:T(8,128)(2,1)S(1)} %pad_maximum_fusion.1), channel_id=1, source_target_pairs={{8,0},{16,8},{24,16},{28,24},{20,28},{12,20},{4,12},{0,4},{9,1},{1... | collective-permute-start | bytes 221192 | tf_op jit(solution)/shard_map/ppermute | solution.py:48
  8.5 28.9 %collective-permute-start = (bf16[96,1152]{1,0:T(8,128)(2,1)S(1)}, bf16[96,1152]{1,0:T(8,128)(2,1)S(1)}, u32[]{:S(2)}, u32[]{:S(2)}) collective-permute-start(bf16[96,1152]{1,0:T(8,128)(2,1)S(1)} %concatenate.32), channel_id=1, source_target_pairs={{0,8},{8,16},{16,24},{24,28},{28,20},{20,12},{12,4},{4,0},{1,9},{9... | collective-permute-start | bytes 663560 | tf_op jit(solution)/shard_map/ppermute | solution.py:44
  10.7 7.6 %copy-start.63 = (s32[8]{0:T(128)S(1)}, s32[8]{0:T(128)}, u32[]{:S(2)}) copy-start(s32[8]{0:T(128)} %constant.390.clone) | copy-start | bytes 100
  10.8 12.8 %copy-start.47 = (s32[8]{0:T(128)S(1)}, s32[8]{0:T(128)}, u32[]{:S(2)}) copy-start(s32[8]{0:T(128)} %constant.391.clone) | copy-start | bytes 100
  10.8 18.6 %copy-start.59 = (f32[192]{0:T(256)S(1)}, f32[192]{0:T(256)}, u32[]{:S(2)}) copy-start(f32[192]{0:T(256)} %param.35) | copy-start | bytes 2308
  10.8 18.6 %copy-start.60 = (f32[192]{0:T(256)S(1)}, f32[192]{0:T(256)}, u32[]{:S(2)}) copy-start(f32[192]{0:T(256)} %param.38) | copy-start | bytes 2308
  16.1 16.4 %collective-permute-start.9 = (bf16[96,384]{0,1:T(8,128)(2,1)}, bf16[96,384]{0,1:T(8,128)(2,1)}, u32[]{:S(2)}, u32[]{:S(2)}) collective-permute-start(bf16[96,384]{0,1:T(8,128)(2,1)} %collective-permute-done.7), channel_id=1, source_target_pairs={{0,8},{8,16},{16,24},{24,28},{28,20},{20,12},{12,4},{4,0},{1,9},{9... | collective-permute-start | bytes 221192 | tf_op jit(solution)/shard_map/ppermute | solution.py:44
  18.3 17.5 %collective-permute-start.10 = (bf16[96,384]{0,1:T(8,128)(2,1)}, bf16[96,384]{0,1:T(8,128)(2,1)}, u32[]{:S(2)}, u32[]{:S(2)}) collective-permute-start(bf16[96,384]{0,1:T(8,128)(2,1)} %collective-permute-done.8), channel_id=1, source_target_pairs={{8,0},{16,8},{24,16},{28,24},{20,28},{12,20},{4,12},{0,4},{9,1},{1... | collective-permute-start | bytes 221192 | tf_op jit(solution)/shard_map/ppermute | solution.py:48
  32.6 28.6 %collective-permute-start.16 = (bf16[96,1536]{1,0:T(8,128)(2,1)S(1)}, bf16[96,1536]{1,0:T(8,128)(2,1)}, u32[]{:S(2)}, u32[]{:S(2)}) collective-permute-start(bf16[96,1536]{1,0:T(8,128)(2,1)S(1)} %constant_dynamic-update-slice_fusion), channel_id=1, source_target_pairs={{0,8},{8,16},{16,24},{24,28},{28,20},{20,12},{12,4},{4,0},{1,9},{9... | collective-permute-start | bytes 884744 | tf_op jit(solution)/shard_map/ppermute | solution.py:44
  35.8 6.8 %collective-permute-start.1 = (bf16[96,1152]{1,0:T(8,128)(2,1)S(1)}, bf16[96,1152]{1,0:T(8,128)(2,1)}, u32[]{:S(2)}, u32[]{:S(2)}) collective-permute-start(bf16[96,1152]{1,0:T(8,128)(2,1)S(1)} %concatenate.32), channel_id=1, source_target_pairs={{8,0},{16,8},{24,16},{28,24},{20,28},{12,20},{4,12},{0,4},{9,1},{1... | collective-permute-start | bytes 663560 | tf_op jit(solution)/shard_map/ppermute | solution.py:48
  37.4 6.2 %collective-permute-start.11 = (bf16[96,384]{0,1:T(8,128)(2,1)}, bf16[96,384]{0,1:T(8,128)(2,1)S(1)}, u32[]{:S(2)}, u32[]{:S(2)}) collective-permute-start(bf16[96,384]{0,1:T(8,128)(2,1)} %collective-permute-done.9), channel_id=1, source_target_pairs={{0,8},{8,16},{16,24},{24,28},{28,20},{20,12},{12,4},{4,0},{1,9},{9... | collective-permute-start | bytes 221192 | tf_op jit(solution)/shard_map/ppermute | solution.py:44
  42.6 5.1 %collective-permute-start.12 = (bf16[96,384]{0,1:T(8,128)(2,1)}, bf16[96,384]{0,1:T(8,128)(2,1)}, u32[]{:S(2)}, u32[]{:S(2)}) collective-permute-start(bf16[96,384]{0,1:T(8,128)(2,1)} %collective-permute-done.10), channel_id=1, source_target_pairs={{8,0},{16,8},{24,16},{28,24},{20,28},{12,20},{4,12},{0,4},{9,1},{1... | collective-permute-start | bytes 221192 | tf_op jit(solution)/shard_map/ppermute | solution.py:48
  43.6 19.6 %collective-permute-start.17 = (bf16[96,1536]{1,0:T(8,128)(2,1)S(1)}, bf16[96,1536]{1,0:T(8,128)(2,1)}, u32[]{:S(2)}, u32[]{:S(2)}) collective-permute-start(bf16[96,1536]{1,0:T(8,128)(2,1)S(1)} %constant_dynamic-update-slice_fusion), channel_id=1, source_target_pairs={{8,0},{16,8},{24,16},{28,24},{20,28},{12,20},{4,12},{0,4},{9,1},{1... | collective-permute-start | bytes 884744 | tf_op jit(solution)/shard_map/ppermute | solution.py:48
  47.6 19.0 %collective-permute-start.2 = (bf16[96,1152]{1,0:T(8,128)(2,1)S(1)}, bf16[96,1152]{1,0:T(8,128)(2,1)S(1)}, u32[]{:S(2)}, u32[]{:S(2)}) collective-permute-start(bf16[96,1152]{1,0:T(8,128)(2,1)S(1)} %collective-permute-done), channel_id=1, source_target_pairs={{0,8},{8,16},{16,24},{24,28},{28,20},{20,12},{12,4},{4,0},{1,9},{9... | collective-permute-start | bytes 663560 | tf_op jit(solution)/shard_map/ppermute | solution.py:44
  51.2 15.8 %collective-permute-start.3 = (bf16[96,1152]{1,0:T(8,128)(2,1)}, bf16[96,1152]{1,0:T(8,128)(2,1)}, u32[]{:S(2)}, u32[]{:S(2)}) collective-permute-start(bf16[96,1152]{1,0:T(8,128)(2,1)} %collective-permute-done.1), channel_id=1, source_target_pairs={{8,0},{16,8},{24,16},{28,24},{20,28},{12,20},{4,12},{0,4},{9,1},{1... | collective-permute-start | bytes 663560 | tf_op jit(solution)/shard_map/ppermute | solution.py:48
  53.0 5.7 %collective-permute-start.13 = (bf16[96,384]{0,1:T(8,128)(2,1)S(1)}, bf16[96,384]{0,1:T(8,128)(2,1)S(1)}, u32[]{:S(2)}, u32[]{:S(2)}) collective-permute-start(bf16[96,384]{0,1:T(8,128)(2,1)S(1)} %collective-permute-done.11), channel_id=1, source_target_pairs={{0,8},{8,16},{16,24},{24,28},{28,20},{20,12},{12,4},{4,0},{1,9},{9... | collective-permute-start | bytes 221192 | tf_op jit(solution)/shard_map/ppermute | solution.py:44
  58.7 11.0 %collective-permute-start.25 = (bf16[96,1536]{1,0:T(8,128)(2,1)}, bf16[96,1536]{1,0:T(8,128)(2,1)}, u32[]{:S(2)}, u32[]{:S(2)}) collective-permute-start(bf16[96,1536]{1,0:T(8,128)(2,1)} %collective-permute-done.23), channel_id=1, source_target_pairs={{0,8},{8,16},{16,24},{24,28},{28,20},{20,12},{12,4},{4,0},{1,9},{9... | collective-permute-start | bytes 884744 | tf_op jit(solution)/shard_map/ppermute | solution.py:44
  61.2 17.2 %collective-permute-start.26 = (bf16[96,1536]{1,0:T(8,128)(2,1)}, bf16[96,1536]{1,0:T(8,128)(2,1)}, u32[]{:S(2)}, u32[]{:S(2)}) collective-permute-start(bf16[96,1536]{1,0:T(8,128)(2,1)} %collective-permute-done.24), channel_id=1, source_target_pairs={{8,0},{16,8},{24,16},{28,24},{20,28},{12,20},{4,12},{0,4},{9,1},{1... | collective-permute-start | bytes 884744 | tf_op jit(solution)/shard_map/ppermute | solution.py:48
  63.2 12.1 %collective-permute-start.18 = (bf16[96,1536]{1,0:T(8,128)(2,1)}, bf16[96,1536]{1,0:T(8,128)(2,1)}, u32[]{:S(2)}, u32[]{:S(2)}) collective-permute-start(bf16[96,1536]{1,0:T(8,128)(2,1)} %collective-permute-done.16), channel_id=1, source_target_pairs={{0,8},{8,16},{16,24},{24,28},{28,20},{20,12},{12,4},{4,0},{1,9},{9... | collective-permute-start | bytes 884744 | tf_op jit(solution)/shard_map/ppermute | solution.py:44
  66.6 15.8 %collective-permute-start.19 = (bf16[96,1536]{1,0:T(8,128)(2,1)}, bf16[96,1536]{1,0:T(8,128)(2,1)}, u32[]{:S(2)}, u32[]{:S(2)}) collective-permute-start(bf16[96,1536]{1,0:T(8,128)(2,1)} %collective-permute-done.17), channel_id=1, source_target_pairs={{8,0},{16,8},{24,16},{28,24},{20,28},{12,20},{4,12},{0,4},{9,1},{1... | collective-permute-start | bytes 884744 | tf_op jit(solution)/shard_map/ppermute | solution.py:48
  67.0 15.4 %collective-permute-start.4 = (bf16[96,1152]{1,0:T(8,128)(2,1)S(1)}, bf16[96,1152]{1,0:T(8,128)(2,1)S(1)}, u32[]{:S(2)}, u32[]{:S(2)}) collective-permute-start(bf16[96,1152]{1,0:T(8,128)(2,1)S(1)} %collective-permute-done.2), channel_id=1, source_target_pairs={{0,8},{8,16},{16,24},{24,28},{28,20},{20,12},{12,4},{4,0},{1,9},{9... | collective-permute-start | bytes 663560 | tf_op jit(solution)/shard_map/ppermute | solution.py:44
  69.7 21.0 %copy-start.24 = (bf16[512,768]{1,0:T(8,128)(2,1)S(1)}, bf16[512,768]{1,0:T(8,128)(2,1)}, u32[]{:S(2)}) copy-start(bf16[512,768]{1,0:T(8,128)(2,1)} %param.32) | copy-start | bytes 2359300
  69.7 13.0 %collective-permute-start.5 = (bf16[96,1152]{1,0:T(8,128)(2,1)}, bf16[96,1152]{1,0:T(8,128)(2,1)S(1)}, u32[]{:S(2)}, u32[]{:S(2)}) collective-permute-start(bf16[96,1152]{1,0:T(8,128)(2,1)} %collective-permute-done.3), channel_id=1, source_target_pairs={{8,0},{16,8},{24,16},{28,24},{20,28},{12,20},{4,12},{0,4},{9,1},{1... | collective-permute-start | bytes 663560 | tf_op jit(solution)/shard_map/ppermute | solution.py:48
  75.3 31.8 %collective-permute-start.27 = (bf16[96,1536]{1,0:T(8,128)(2,1)}, bf16[96,1536]{1,0:T(8,128)(2,1)}, u32[]{:S(2)}, u32[]{:S(2)}) collective-permute-start(bf16[96,1536]{1,0:T(8,128)(2,1)} %collective-permute-done.25), channel_id=1, source_target_pairs={{0,8},{8,16},{16,24},{24,28},{28,20},{20,12},{12,4},{4,0},{1,9},{9... | collective-permute-start | bytes 884744 | tf_op jit(solution)/shard_map/ppermute | solution.py:44
  78.4 31.8 %collective-permute-start.20 = (bf16[96,1536]{1,0:T(8,128)(2,1)}, bf16[96,1536]{1,0:T(8,128)(2,1)}, u32[]{:S(2)}, u32[]{:S(2)}) collective-permute-start(bf16[96,1536]{1,0:T(8,128)(2,1)} %collective-permute-done.18), channel_id=1, source_target_pairs={{0,8},{8,16},{16,24},{24,28},{28,20},{20,12},{12,4},{4,0},{1,9},{9... | collective-permute-start | bytes 884744 | tf_op jit(solution)/shard_map/ppermute | solution.py:44
  82.4 31.5 %collective-permute-start.28 = (bf16[96,1536]{1,0:T(8,128)(2,1)}, bf16[96,1536]{1,0:T(8,128)(2,1)}, u32[]{:S(2)}, u32[]{:S(2)}) collective-permute-start(bf16[96,1536]{1,0:T(8,128)(2,1)} %collective-permute-done.26), channel_id=1, source_target_pairs={{8,0},{16,8},{24,16},{28,24},{20,28},{12,20},{4,12},{0,4},{9,1},{1... | collective-permute-start | bytes 884744 | tf_op jit(solution)/shard_map/ppermute | solution.py:48
  82.4 31.5 %collective-permute-start.21 = (bf16[96,1536]{1,0:T(8,128)(2,1)}, bf16[96,1536]{1,0:T(8,128)(2,1)}, u32[]{:S(2)}, u32[]{:S(2)}) collective-permute-start(bf16[96,1536]{1,0:T(8,128)(2,1)} %collective-permute-done.19), channel_id=1, source_target_pairs={{8,0},{16,8},{24,16},{28,24},{20,28},{12,20},{4,12},{0,4},{9,1},{1... | collective-permute-start | bytes 884744 | tf_op jit(solution)/shard_map/ppermute | solution.py:48
  82.8 7.9 %collective-permute-start.6 = (bf16[96,1152]{1,0:T(8,128)(2,1)S(1)}, bf16[96,1152]{1,0:T(8,128)(2,1)S(1)}, u32[]{:S(2)}, u32[]{:S(2)}) collective-permute-start(bf16[96,1152]{1,0:T(8,128)(2,1)S(1)} %collective-permute-done.4), channel_id=1, source_target_pairs={{0,8},{8,16},{16,24},{24,28},{28,20},{20,12},{12,4},{4,0},{1,9},{9... | collective-permute-start | bytes 663560 | tf_op jit(solution)/shard_map/ppermute | solution.py:44
  105.3 10.5 %collective-permute-start.14 = (bf16[2,2,128,768]{3,2,1,0:T(8,128)(2,1)S(1)}, bf16[2,2,128,768]{3,2,1,0:T(8,128)(2,1)S(1)}, u32[]{:S(2)}, u32[]{:S(2)}) collective-permute-start(bf16[2,2,128,768]{3,2,1,0:T(8,128)(2,1)S(1)} %fusion.39), channel_id=1, source_target_pairs={{0,1},{1,0},{2,3},{3,2},{4,5},{5,4},{6,7},{7,6},{8,9},{9,8},{10,11... | collective-permute-start | bytes 2359304 | tf_op jit(solution)/shard_map/ppermute | solution.py:66
  107.1 16.7 %collective-permute-start.29 = (bf16[96,1536]{1,0:T(8,128)(2,1)}, bf16[96,1536]{1,0:T(8,128)(2,1)S(1)}, u32[]{:S(2)}, u32[]{:S(2)}) collective-permute-start(bf16[96,1536]{1,0:T(8,128)(2,1)} %collective-permute-done.27), channel_id=1, source_target_pairs={{0,8},{8,16},{16,24},{24,28},{28,20},{20,12},{12,4},{4,0},{1,9},{9... | collective-permute-start | bytes 884744 | tf_op jit(solution)/shard_map/ppermute | solution.py:44
  110.2 12.8 %collective-permute-start.22 = (bf16[96,1536]{1,0:T(8,128)(2,1)}, bf16[96,1536]{1,0:T(8,128)(2,1)S(1)}, u32[]{:S(2)}, u32[]{:S(2)}) collective-permute-start(bf16[96,1536]{1,0:T(8,128)(2,1)} %collective-permute-done.20), channel_id=1, source_target_pairs={{0,8},{8,16},{16,24},{24,28},{28,20},{20,12},{12,4},{4,0},{1,9},{9... | collective-permute-start | bytes 884744 | tf_op jit(solution)/shard_map/ppermute | solution.py:44
  116.0 11.0 %collective-permute-start.15 = (bf16[2,1,128,768]{3,2,1,0:T(8,128)(2,1)S(1)}, bf16[2,1,128,768]{3,2,1,0:T(8,128)(2,1)S(1)}, u32[]{:S(2)}, u32[]{:S(2)}) collective-permute-start(bf16[2,1,128,768]{3,2,1,0:T(8,128)(2,1)S(1)} %constant_dynamic-slice_fusion), channel_id=1, source_target_pairs={{0,2},{1,3},{2,0},{3,1},{4,6},{5,7},{6,4},{7,5},{8,10},{9,11},{10,... | collective-permute-start | bytes 1179656 | tf_op jit(solution)/shard_map/ppermute | solution.py:66
  127.7 9.0 %copy-start.52 = (f32[128]{0:T(128)}, f32[128]{0:T(128)S(1)}, u32[]{:S(2)}) copy-start(f32[128]{0:T(128)S(1)} %get-tuple-element.79) | copy-start | bytes 1540
  163.6 2.4 collective-permute-start.30
  166.2 11.6 %copy-start.56 = (f32[768]{0:T(1024)S(1)}, f32[768]{0:T(1024)}, u32[]{:S(2)}) copy-start(f32[768]{0:T(1024)} %param.46) | copy-start | bytes 9220
  166.2 11.4 %collective-permute-start.31 = (bf16[2,1,128,768]{3,2,1,0:T(8,128)(2,1)S(1)}, bf16[2,1,128,768]{3,2,1,0:T(8,128)(2,1)S(1)}, u32[]{:S(2)}, u32[]{:S(2)}) collective-permute-start(bf16[2,1,128,768]{3,2,1,0:T(8,128)(2,1)S(1)} %constant_dynamic-slice_fusion.1), channel_id=1, source_target_pairs={{0,2},{1,3},{2,0},{3,1},{4,6},{5,7},{6,4},{7,5},{8,10},{9,11},{10,... | collective-permute-start | bytes 1179656 | tf_op jit(solution)/shard_map/ppermute | solution.py:66
  178.5 9.0 %copy-start.68 = (f32[512,768]{1,0:T(8,128)S(1)}, f32[512,768]{1,0:T(8,128)}, u32[]{:S(2)}) copy-start(f32[512,768]{1,0:T(8,128)} %get-tuple-element.72) | copy-start | bytes 4718596
  193.2 10.0 %copy-start.53 = (f32[128]{0:T(128)S(1)}, f32[128]{0:T(128)}, u32[]{:S(2)}) copy-start(f32[128]{0:T(128)} %copy-done.52) | copy-start | bytes 1540
  193.2 1.8 collective-permute-start.32
  195.1 7.2 %collective-permute-start.33 = (bf16[1,1,128,768]{3,2,1,0:T(8,128)(2,1)S(1)}, bf16[1,1,128,768]{3,2,1,0:T(8,128)(2,1)S(1)}, u32[]{:S(2)}, u32[]{:S(2)}) collective-permute-start(bf16[1,1,128,768]{3,2,1,0:T(8,128)(2,1)S(1)} %constant_dynamic-slice_fusion.2), channel_id=1, source_target_pairs={{0,2},{1,3},{2,0},{3,1},{4,6},{5,7},{6,4},{7,5},{8,10},{9,11},{10,... | collective-permute-start | bytes 589832 | tf_op jit(solution)/shard_map/ppermute | solution.py:66
  204.0 5.1 %collective-permute-start.34 = (bf16[128,768]{1,0:T(8,128)(2,1)S(1)}, bf16[128,768]{1,0:T(8,128)(2,1)S(1)}, u32[]{:S(2)}, u32[]{:S(2)}) collective-permute-start(bf16[128,768]{1,0:T(8,128)(2,1)S(1)} %convert_element_type.276), channel_id=1, source_target_pairs={{0,1},{1,2},{2,3},{3,0},{4,5},{5,6},{6,7},{7,4},{8,9},{9,10},{10,1... | collective-permute-start | bytes 589832 | tf_op jit(solution)/shard_map/ppermute | solution.py:201
  209.1 5.6 %collective-permute-start.35 = (bf16[128,768]{1,0:T(8,128)(2,1)S(1)}, bf16[128,768]{1,0:T(8,128)(2,1)S(1)}, u32[]{:S(2)}, u32[]{:S(2)}) collective-permute-start(bf16[128,768]{1,0:T(8,128)(2,1)S(1)} %collective-permute-done.34), channel_id=1, source_target_pairs={{0,1},{1,2},{2,3},{3,0},{4,5},{5,6},{6,7},{7,4},{8,9},{9,10},{10,1... | collective-permute-start | bytes 589832 | tf_op jit(solution)/shard_map/ppermute | solution.py:201
  209.1 5.9 %collective-permute-start.36 = (bf16[128,768]{1,0:T(8,128)(2,1)S(1)}, bf16[128,768]{1,0:T(8,128)(2,1)S(1)}, u32[]{:S(2)}, u32[]{:S(2)}) collective-permute-start(bf16[128,768]{1,0:T(8,128)(2,1)S(1)} %convert_element_type.276), channel_id=1, source_target_pairs={{0,3},{1,0},{2,1},{3,2},{4,7},{5,4},{6,5},{7,6},{8,11},{9,8},{10,9... | collective-permute-start | bytes 589832 | tf_op jit(solution)/shard_map/ppermute | solution.py:203
  222.2 12.3 %all-to-all-start.1 = ((f32[8,47,128]{2,1,0:T(8,128)}), f32[8,47,128]{2,1,0:T(8,128)S(1)}, u32[]{:S(2)}, u32[]{:S(2)}) async-start(f32[8,47,128]{2,1,0:T(8,128)} %broadcast_in_dim.38), calls=%async_computation.1 | async-start | bytes 393216 | tf_op jit(solution)/shard_map/all_to_all | solution.py:237
  225.6 12.4 %copy-start.19 = (bf16[512,768]{1,0:T(8,128)(2,1)S(1)}, bf16[512,768]{1,0:T(8,128)(2,1)}, u32[]{:S(2)}) copy-start(bf16[512,768]{1,0:T(8,128)(2,1)} %copy-done.18) | copy-start | bytes 2359300
  225.6 12.4 %copy-start.65 = (bf16[512,768]{1,0:T(8,128)(2,1)S(1)}, bf16[512,768]{1,0:T(8,128)(2,1)}, u32[]{:S(2)}) copy-start(bf16[512,768]{1,0:T(8,128)(2,1)} %copy-done.64) | copy-start | bytes 2359300
  234.5 15.6 %all-to-all-start.2 = ((bf16[8,96,192]{1,2,0:T(8,128)(2,1)}), bf16[8,96,192]{1,2,0:T(8,128)(2,1)S(1)}, u32[]{:S(2)}, u32[]{:S(2)}) async-start(bf16[8,96,192]{1,2,0:T(8,128)(2,1)} %copy.177), calls=%async_computation.2 | async-start | bytes 786432 | tf_op jit(solution)/shard_map/all_to_all | solution.py:225
  239.9 14.6 %copy-start.17 = (bf16[512,768]{1,0:T(8,128)(2,1)S(1)}, bf16[512,768]{1,0:T(8,128)(2,1)}, u32[]{:S(2)}) copy-start(bf16[512,768]{1,0:T(8,128)(2,1)} %copy-done.16) | copy-start | bytes 2359300
  239.9 14.6 %copy-start.67 = (bf16[512,768]{1,0:T(8,128)(2,1)S(1)}, bf16[512,768]{1,0:T(8,128)(2,1)}, u32[]{:S(2)}) copy-start(bf16[512,768]{1,0:T(8,128)(2,1)} %copy-done.66) | copy-start | bytes 2359300
  250.9 32.4 %all-to-all-start.4 = ((bf16[8,96,768]{2,1,0:T(8,128)(2,1)}), bf16[8,96,768]{2,1,0:T(8,128)(2,1)S(1)}, u32[]{:S(2)}, u32[]{:S(2)}) async-start(bf16[8,96,768]{2,1,0:T(8,128)(2,1)} %bitcast.61), calls=%async_computation.4 | async-start | bytes 2359296 | tf_op jit(solution)/shard_map/all_to_all | solution.py:225
  256.4 30.5 %copy-start.22 = (bf16[128,768]{1,0:T(8,128)(2,1)S(1)}, bf16[128,768]{1,0:T(8,128)(2,1)}, u32[]{:S(2)}) copy-start(bf16[128,768]{1,0:T(8,128)(2,1)} %get-tuple-element.45) | copy-start | bytes 589828
  283.3 42.5 %all-to-all-start.3 = ((bf16[8,96,768]{2,1,0:T(8,128)(2,1)}), bf16[8,96,768]{2,1,0:T(8,128)(2,1)S(1)}, u32[]{:S(2)}, u32[]{:S(2)}) async-start(bf16[8,96,768]{2,1,0:T(8,128)(2,1)} %bitcast.249), calls=%async_computation.3 | async-start | bytes 2359296 | tf_op jit(solution)/shard_map/all_to_all | solution.py:225
  286.9 18.2 %copy-start.3 = (bf16[768,1152]{1,0:T(8,128)(2,1)S(1)}, bf16[768,1152]{1,0:T(8,128)(2,1)}, u32[]{:S(2)}) copy-start(bf16[768,1152]{1,0:T(8,128)(2,1)} %copy-done.2) | copy-start | bytes 5308420
  308.8 23.0 %collective-permute-start.37 = (bf16[1,2,128,768]{3,2,1,0:T(8,128)(2,1)}, bf16[1,2,128,768]{3,2,1,0:T(8,128)(2,1)}, u32[]{:S(2)}, u32[]{:S(2)}) collective-permute-start(bf16[1,2,128,768]{3,2,1,0:T(8,128)(2,1)} %dynamic-slice_bitcast_fusion), channel_id=1, source_target_pairs={{0,1},{1,0},{2,3},{3,2},{4,5},{5,4},{6,7},{7,6},{8,9},{9,8},{10,11... | collective-permute-start | bytes 1179656 | tf_op jit(solution)/shard_map/ppermute | solution.py:66
  325.8 31.0 %all-to-all-start = ((bf16[8,96,576]{2,1,0:T(8,128)(2,1)}), bf16[8,96,576]{2,1,0:T(8,128)(2,1)}, u32[]{:S(2)}, u32[]{:S(2)}) async-start(bf16[8,96,576]{2,1,0:T(8,128)(2,1)} %bitcast.241), calls=%async_computation | async-start | bytes 1966080 | tf_op jit(solution)/shard_map/all_to_all | solution.py:225
  333.1 6.9 %collective-permute-start.38 = (bf16[1,1,128,768]{3,2,1,0:T(8,128)(2,1)S(1)}, bf16[1,1,128,768]{3,2,1,0:T(8,128)(2,1)S(1)}, u32[]{:S(2)}, u32[]{:S(2)}) collective-permute-start(bf16[1,1,128,768]{3,2,1,0:T(8,128)(2,1)S(1)} %constant_dynamic-slice_fusion.3), channel_id=1, source_target_pairs={{0,2},{1,3},{2,0},{3,1},{4,6},{5,7},{6,4},{7,5},{8,10},{9,11},{10,... | collective-permute-start | bytes 589832 | tf_op jit(solution)/shard_map/ppermute | solution.py:66
  349.2 9.7 %copy-start = (bf16[512,768]{1,0:T(8,128)(2,1)S(1)}, bf16[512,768]{1,0:T(8,128)(2,1)}, u32[]{:S(2)}) copy-start(bf16[512,768]{1,0:T(8,128)(2,1)} %all_gather.26) | copy-start | bytes 2359300
  350.1 9.7 %copy-start.1 = (bf16[512,768]{1,0:T(8,128)(2,1)S(1)}, bf16[512,768]{1,0:T(8,128)(2,1)}, u32[]{:S(2)}) copy-start(bf16[512,768]{1,0:T(8,128)(2,1)} %all_gather.28) | copy-start | bytes 2359300
  (49 other events, 139.1 us)
